TPU v7x, 32 devices: a whole 2x2x4 slice. The times are simulated.
32 devices in a mesh: seq: 16 (over z, x, core), pipe: 2 (over y).
Axes of the slice: x: 2, y: 2, z: 4, core: 2. Of those that a mesh axis runs over, the one named last changes fastest.
Arguments:
- queries: bfloat16 [2, 32, 2048, 128], P('pipe', None, 'seq'), may hold values from -160 to 160
- key_states: bfloat16 [2, 4, 2048, 128], P('pipe', None, 'seq'), may hold values from -5 to 5
- value_states: bfloat16 [2, 4, 2048, 128], P('pipe', None, 'seq'), may hold values from -6 to 6
- outputs: bfloat16 [2, 32, 2048, 128], P('pipe', None, 'seq'), may hold values from -6 to 6
- out_grads: bfloat16 [2, 32, 2048, 128], P('pipe', None, 'seq'), may hold values from -6 to 6
- selected: int32 [2, 4, 4, 2], P('pipe'), may hold values from 0 to 2, as said below
Outputs:
- grad_queries: bfloat16 [2, 32, 2048, 128], P('pipe', None, 'seq')
- grad_keys: bfloat16 [2, 4, 2048, 128], P('pipe', None, 'seq')
- grad_values: bfloat16 [2, 4, 2048, 128], P('pipe', None, 'seq')
Inputs may be any that keep to these rules, and one draw needn't show every extreme that they name: `selected`: for every block b of 2 or more and every key head the two entries are different blocks below b. For block 1 the entries are 0 and 1, for block 0 both are 0. An entry that is not below its block's index stands for no block.
All inputs are finite; a program needn't handle non-finite values.
Results may differ from a plain program's by a relative error of at most 0.009.
Values may be sent and summed in bfloat16 or wider, within the bound.
No kernel may reach another device: no remote copies, remote signals or barrier semaphores. Data moves between devices by JAX's collectives and lax.ppermute only.
A program may use at most 64 MiB of HBM per device.

v0:
```python
import jax
import jax.numpy as jnp
from jax import lax
from jax.sharding import PartitionSpec as P

BLK = 512


NEG_FILL = -1e30


def shifted(block, axis, distance):
    devices = range(lax.axis_size(axis))
    route = [(i - distance, i) for i in devices if i - distance in devices]
    return lax.ppermute(block, axis, route)


def head_layout(tensor, targets, heads_here, pair_count, piece_rows):
    trailing = tensor.shape[2:]
    shaped = tensor.reshape((targets // 2, heads_here, pair_count, 2, piece_rows) + trailing)
    order = (0, 3, 1, 2, 4) + tuple(range(5, 5 + len(trailing)))
    return shaped.transpose(order).reshape(
        (targets, heads_here, pair_count * piece_rows) + trailing
    )


def allowed_mask(positions, own_length, first_ok, second_ok):
    columns = jnp.arange(2 * BLK + own_length)
    own_mask = columns[None, :] - 2 * BLK <= positions[:, None]
    picked = jnp.where(columns < BLK, first_ok, second_ok)
    return jnp.where(columns[None, :] < 2 * BLK, picked[None, :], own_mask)


def attend_rows(query_rows, grad_rows, delta_rows, key_rows, value_rows, allowed, scaling):
    scores = (
        jnp.einsum("hnd,ld->hnl", query_rows, key_rows, preferred_element_type=jnp.float32)
        * scaling
    )
    scores = jnp.where(allowed[None], scores, NEG_FILL)
    row_max = jnp.max(scores, axis=-1, keepdims=True)
    weights_raw = jnp.exp(scores - row_max)
    probs = weights_raw / jnp.sum(weights_raw, axis=-1, keepdims=True)
    probs_low = probs.astype(jnp.bfloat16)
    dprobs = jnp.einsum("hnd,ld->hnl", grad_rows, value_rows, preferred_element_type=jnp.float32)
    dscores = (probs * (dprobs - delta_rows.astype(jnp.float32)[..., None])).astype(jnp.bfloat16)
    query_grad = (
        jnp.einsum("hnl,ld->hnd", dscores, key_rows, preferred_element_type=jnp.float32) * scaling
    )
    key_grad = (
        jnp.einsum("hnl,hnd->ld", dscores, query_rows, preferred_element_type=jnp.float32) * scaling
    )
    value_grad = jnp.einsum("hnl,hnd->ld", probs_low, grad_rows, preferred_element_type=jnp.float32)
    return (query_grad, key_grad, value_grad)


def add_rows(running, term, start):
    current = lax.dynamic_slice_in_dim(running, start, term.shape[0], 0)
    return lax.dynamic_update_slice_in_dim(running, current + term, start, 0)


def settle(
    query_back,
    key_back,
    value_back,
    head_count,
    key_heads,
    heads_here,
    pair_count,
    piece_rows,
    targets,
):
    feature = query_back.shape[-1]
    local_tokens = 2 * pair_count * piece_rows
    query_out = query_back.reshape(targets // 2, 2, heads_here, pair_count, piece_rows, feature)
    query_out = query_out.transpose(0, 2, 3, 1, 4, 5).reshape(1, head_count, local_tokens, feature)

    def fold_group(back):
        grouped = back.reshape(key_heads, targets // key_heads, local_tokens, feature).astype(
            jnp.float32
        )
        return jnp.sum(grouped, axis=1).astype(jnp.bfloat16)[None]

    return (query_out, fold_group(key_back), fold_group(value_back))


def on_device(queries, key_states, value_states, outputs, out_grads, selected):
    targets = lax.axis_size("seq")
    head_count = queries.shape[1]
    key_heads = key_states.shape[1]
    local_tokens = queries.shape[2]
    feature = queries.shape[3]
    piece_rows = BLK // 8
    pair_count = local_tokens // (2 * piece_rows)
    heads_here = 2 * head_count // targets
    scaling = feature ** (-0.5)
    half_block = BLK // 2
    quarter = BLK // 4
    deltas = jnp.sum(
        out_grads[0].astype(jnp.float32) * outputs[0].astype(jnp.float32), axis=-1
    ).astype(jnp.bfloat16)
    query_send = head_layout(queries[0], targets, heads_here, pair_count, piece_rows)
    grad_send = head_layout(out_grads[0], targets, heads_here, pair_count, piece_rows)
    delta_send = head_layout(deltas, targets, heads_here, pair_count, piece_rows)
    key_send = jnp.repeat(key_states[0], targets // key_heads, axis=0)
    value_send = jnp.repeat(value_states[0], targets // key_heads, axis=0)
    rows_each = heads_here * pair_count * piece_rows
    packed = jnp.concatenate(
        [
            query_send.reshape(targets, rows_each, feature),
            grad_send.reshape(targets, rows_each, feature),
            key_send,
            value_send,
        ],
        axis=1,
    )
    received, delta_back = (
        lax.all_to_all(packed, "seq", split_axis=0, concat_axis=1, tiled=True),
        lax.all_to_all(
            delta_send.reshape(targets, rows_each), "seq", split_axis=0, concat_axis=1, tiled=True
        ),
    )
    received = received.reshape(targets, 2 * rows_each + 2 * local_tokens, feature)

    def unpack(portion):
        shaped = portion.reshape(targets, heads_here, pair_count * piece_rows, feature)
        return shaped.transpose(1, 0, 2, 3).reshape(
            heads_here, targets * pair_count * piece_rows, feature
        )

    query_head = unpack(received[:, :rows_each])
    grad_head = unpack(received[:, rows_each : 2 * rows_each])
    key_full = received[:, 2 * rows_each : 2 * rows_each + local_tokens].reshape(
        targets * local_tokens, feature
    )
    value_full = received[:, 2 * rows_each + local_tokens :].reshape(
        targets * local_tokens, feature
    )
    delta_head = (
        delta_back.reshape(targets, heads_here, pair_count * piece_rows)
        .transpose(1, 0, 2)
        .reshape(heads_here, targets * pair_count * piece_rows)
    )
    seq_rank = lax.axis_index("seq")
    head_group = seq_rank // 2 * heads_here // (head_count // key_heads)
    parity = seq_rank % 2
    chosen = lax.dynamic_index_in_dim(selected[0], head_group, axis=1, keepdims=False)
    row_ids = jnp.arange(half_block)
    positions = (
        2 * piece_rows * (row_ids // piece_rows) + piece_rows * parity + row_ids % piece_rows
    )
    block_total = key_full.shape[0] // BLK

    def step(block_num, running):
        query_acc, key_acc, value_acc = running
        first_pick = chosen[block_num, 0]
        second_pick = chosen[block_num, 1]
        first_ok = first_pick < block_num
        second_ok = second_pick < block_num
        key_first = lax.dynamic_slice_in_dim(key_full, first_pick * BLK, BLK, 0)
        key_second = lax.dynamic_slice_in_dim(key_full, second_pick * BLK, BLK, 0)
        key_own = lax.dynamic_slice_in_dim(key_full, block_num * BLK, BLK, 0)
        value_first = lax.dynamic_slice_in_dim(value_full, first_pick * BLK, BLK, 0)
        value_second = lax.dynamic_slice_in_dim(value_full, second_pick * BLK, BLK, 0)
        value_own = lax.dynamic_slice_in_dim(value_full, block_num * BLK, BLK, 0)
        query_block = lax.dynamic_slice_in_dim(query_head, block_num * half_block, half_block, 1)
        grad_block = lax.dynamic_slice_in_dim(grad_head, block_num * half_block, half_block, 1)
        delta_block = lax.dynamic_slice_in_dim(delta_head, block_num * half_block, half_block, 1)
        low_keys = jnp.concatenate([key_first, key_second, key_own[:half_block]], axis=0)
        low_values = jnp.concatenate([value_first, value_second, value_own[:half_block]], axis=0)
        high_keys = jnp.concatenate([key_first, key_second, key_own], axis=0)
        high_values = jnp.concatenate([value_first, value_second, value_own], axis=0)
        low_mask = allowed_mask(positions[:quarter], half_block, first_ok, second_ok)
        high_mask = allowed_mask(positions[quarter:], BLK, first_ok, second_ok)
        query_low, key_low, value_low = attend_rows(
            query_block[:, :quarter],
            grad_block[:, :quarter],
            delta_block[:, :quarter],
            low_keys,
            low_values,
            low_mask,
            scaling,
        )
        query_high, key_high, value_high = attend_rows(
            query_block[:, quarter:],
            grad_block[:, quarter:],
            delta_block[:, quarter:],
            high_keys,
            high_values,
            high_mask,
            scaling,
        )
        query_rows = jnp.concatenate([query_low, query_high], axis=1).astype(jnp.bfloat16)
        query_acc = lax.dynamic_update_slice_in_dim(
            query_acc, query_rows, block_num * half_block, 1
        )
        key_own_grad = key_high[2 * BLK :] + jnp.pad(key_low[2 * BLK :], ((0, half_block), (0, 0)))
        value_own_grad = value_high[2 * BLK :] + jnp.pad(
            value_low[2 * BLK :], ((0, half_block), (0, 0))
        )
        key_acc = add_rows(key_acc, key_low[:BLK] + key_high[:BLK], first_pick * BLK)
        key_acc = add_rows(
            key_acc, key_low[BLK : 2 * BLK] + key_high[BLK : 2 * BLK], second_pick * BLK
        )
        key_acc = add_rows(key_acc, key_own_grad, block_num * BLK)
        value_acc = add_rows(value_acc, value_low[:BLK] + value_high[:BLK], first_pick * BLK)
        value_acc = add_rows(
            value_acc, value_low[BLK : 2 * BLK] + value_high[BLK : 2 * BLK], second_pick * BLK
        )
        value_acc = add_rows(value_acc, value_own_grad, block_num * BLK)
        return (query_acc, key_acc, value_acc)

    query_init = jnp.zeros(query_head.shape, jnp.bfloat16)
    key_init = jnp.zeros(key_full.shape, jnp.float32)
    query_done, key_done, value_done = lax.fori_loop(
        0, block_total, step, (query_init, key_init, key_init)
    )
    query_out_send = query_done.reshape(heads_here, targets, pair_count * piece_rows, feature)
    key_out_send = key_done.astype(jnp.bfloat16).reshape(1, targets, local_tokens, feature)
    value_out_send = value_done.astype(jnp.bfloat16).reshape(1, targets, local_tokens, feature)
    query_back, key_back, value_back = (
        lax.all_to_all(query_out_send, "seq", split_axis=1, concat_axis=0, tiled=True),
        lax.all_to_all(key_out_send, "seq", split_axis=1, concat_axis=0, tiled=True),
        lax.all_to_all(value_out_send, "seq", split_axis=1, concat_axis=0, tiled=True),
    )
    query_out, key_out, value_out = settle(
        query_back,
        key_back,
        value_back,
        head_count,
        key_heads,
        heads_here,
        pair_count,
        piece_rows,
        targets,
    )
    return shifted((query_out, key_out, value_out), "pipe", -1)


def solution(mesh):
    return jax.shard_map(
        on_device,
        mesh=mesh,
        in_specs=(
            P("pipe", None, "seq", None),
            P("pipe", None, "seq", None),
            P("pipe", None, "seq", None),
            P("pipe", None, "seq", None),
            P("pipe", None, "seq", None),
            P("pipe", None, None, None),
        ),
        out_specs=(
            P("pipe", None, "seq", None),
            P("pipe", None, "seq", None),
            P("pipe", None, "seq", None),
        ),
        check_vma=False,
    )
```

profile of v0, /device:TPU:8, one launch (start us, length us, event | category | flops | bytes accessed | tf_op | source)
XLA Modules:
  0.0 328.0 jit_solution(7640857704535869966)
XLA Ops:
  0.7 2.3 multiply_reduce_fusion
  5.0 6.3 %all-to-all-start.1 = ((bf16[16,2,128]{2,1,0:T(2,128)(2,1)}), bf16[16,2,128]{2,1,0:T(2,128)(2,1)S(1)}, u32[]{:S(2)}, u32[]{:S(2)}) async-start(bf16[16,2,128]{2,1,0:T(2,128)(2,1)} %reshape.286), calls=%async_computation.1 | async-start | bytes 16384 | tf_op jit(solution)/shard_map/all_to_all | solution.py:118
  11.7 1.8 pad_maximum_fusion
  13.5 2.7 all-to-all-done.1
  16.2 5.1 %all-to-all-start = ((bf16[16,768,128]{2,1,0:T(8,128)(2,1)}), bf16[16,768,128]{2,1,0:T(8,128)(2,1)S(1)}, u32[]{:S(2)}, u32[]{:S(2)}) async-start(bf16[16,768,128]{2,1,0:T(8,128)(2,1)} %pad_maximum_fusion), calls=%async_computation | async-start | bytes 6291456 | tf_op jit(solution)/shard_map/all_to_all | solution.py:117
  22.3 67.3 %all-to-all-done = bf16[16,768,128]{2,1,0:T(8,128)(2,1)S(1)} async-done(((bf16[16,768,128]{2,1,0:T(8,128)(2,1)}), bf16[16,768,128]{2,1,0:T(8,128)(2,1)S(1)}, u32[]{:S(2)}, u32[]{:S(2)}) %all-to-all-start) | async-done | bytes 3145760 | tf_op jit(solution)/shard_map/all_to_all | solution.py:117
  89.8 1.1 copy.47
  92.9 1.1 broadcast_in_dim.212
  95.2 140.8 %while.20 = (s32[]{:T(128)}, bf16[4,1024,128]{2,1,0:T(8,128)(2,1)}, f32[2048,128]{1,0:T(8,128)S(1)}, f32[2048,128]{1,0:T(8,128)}, s32[4,2]{0,1:T(2,128)S(1)}, /*...) while((s32[]{:T(128)}, bf16[4,1024,128]{2,1,0:T(8,128)(2,1)}, ...), condition=%wide.region_6.7_spmd, body=%wide.region_1.6_spmd.sunk | while | flops 2244659712 | bytes 61977432 | solution.py:214
  99.3 1.1 constant_dynamic-slice_fusion.19
  100.5 3.8 %fusion.170 = (f32[4,128]{1,0:T(4,128)S(1)}, f32[4,128,1536]{2,1,0:T(8,128)}) fusion(pred[128,1536]{1,0:T(8,128)(4,1)S(1)} %compare_select_fusion.4, bf16[4,1024,128]{2,1,0:T(8,128)(2,1)} %get-tuple-element.492, s32[]{:T(128)S(6)} %add.374, bf16[512,128]{1,0:T(8,128)(2,1)S(1)} %get-tuple-element.436, bf16[512,128]{1,0:T(8,128)(2,1)S(1)} %get-tuple-element.437, ...), kind=kOutput, calls=%fused_computation.133.clone.1 | convolution fusion | flops 205653504 | bytes 3868676 | tf_op jit(solution)/shard_map/while/body/eval_jaxpr/sub | solution.py:41
  104.3 1.1 constant_dynamic-slice_fusion.20
  105.4 2.6 fusion.171
  109.7 3.5 %fusion.174 = (f32[4,128]{1,0:T(4,128)S(1)}, f32[4,128,1280]{2,1,0:T(8,128)}) fusion(pred[128,1280]{1,0:T(8,128)(4,1)S(1)} %compare_select_fusion.5, bf16[4,1024,128]{2,1,0:T(8,128)(2,1)} %get-tuple-element.492, s32[]{:T(128)S(6)} %select_n.251, bf16[256,128]{1,0:T(8,128)(2,1)S(1)} %constant_dynamic-slice_fusion.21, ...), kind=kOutput, calls=%fused_computation.134.clone.1 | convolution fusion | flops 171377920 | bytes 3246084 | tf_op jit(solution)/shard_map/while/body/eval_jaxpr/sub | solution.py:41
  114.0 2.4 fusion.175
  116.4 1.1 copy-done.4
  118.8 2.9 convolution_bitcast_fusion.6
  121.7 3.5 %convolution_bitcast_fusion.7 = f32[1280,128]{1,0:T(8,128)} fusion(f32[4,128]{1,0:T(4,128)} %copy-done.17, bf16[4,1024,128]{2,1,0:T(8,128)(2,1)} %get-tuple-element.494, s32[]{:T(128)S(6)} %select_n.251, pred[128,1280]{1,0:T(8,128)(4,1)} %copy-done.10, bf16[4,1024,128]{2,1,0:T(8,128)(2,1)} %get-tuple-element.492, bf16[256,128]{1,0:T(8,128)(2,1)} %copy-done.13, ...), kind=kOutput, calls=%fused_computation.17.clone.1 | convolution fusion | flops 339805952 | bytes 1412096 | tf_op jit(solution)/shard_map/while/body/eval_jaxpr/hnl,hnd->ld/dot_general | solution.py:52
  125.3 1.7 fusion.177
  126.9 1.5 fusion.178
  134.6 1.1 constant_dynamic-slice_fusion.19
  135.7 3.8 %fusion.170 = (f32[4,128]{1,0:T(4,128)S(1)}, f32[4,128,1536]{2,1,0:T(8,128)}) fusion(pred[128,1536]{1,0:T(8,128)(4,1)S(1)} %compare_select_fusion.4, bf16[4,1024,128]{2,1,0:T(8,128)(2,1)} %get-tuple-element.492, s32[]{:T(128)S(6)} %add.374, bf16[512,128]{1,0:T(8,128)(2,1)S(1)} %get-tuple-element.436, bf16[512,128]{1,0:T(8,128)(2,1)S(1)} %get-tuple-element.437, ...), kind=kOutput, calls=%fused_computation.133.clone.1 | convolution fusion | flops 205653504 | bytes 3868676 | tf_op jit(solution)/shard_map/while/body/eval_jaxpr/sub | solution.py:41
  140.6 2.6 fusion.171
  144.9 3.5 %fusion.174 = (f32[4,128]{1,0:T(4,128)S(1)}, f32[4,128,1280]{2,1,0:T(8,128)}) fusion(pred[128,1280]{1,0:T(8,128)(4,1)S(1)} %compare_select_fusion.5, bf16[4,1024,128]{2,1,0:T(8,128)(2,1)} %get-tuple-element.492, s32[]{:T(128)S(6)} %select_n.251, bf16[256,128]{1,0:T(8,128)(2,1)S(1)} %constant_dynamic-slice_fusion.21, ...), kind=kOutput, calls=%fused_computation.134.clone.1 | convolution fusion | flops 171377920 | bytes 3246084 | tf_op jit(solution)/shard_map/while/body/eval_jaxpr/sub | solution.py:41
  149.2 2.4 fusion.175
  151.6 1.1 copy-done.4
  154.0 2.9 convolution_bitcast_fusion.6
  156.9 3.5 %convolution_bitcast_fusion.7 = f32[1280,128]{1,0:T(8,128)} fusion(f32[4,128]{1,0:T(4,128)} %copy-done.17, bf16[4,1024,128]{2,1,0:T(8,128)(2,1)} %get-tuple-element.494, s32[]{:T(128)S(6)} %select_n.251, pred[128,1280]{1,0:T(8,128)(4,1)} %copy-done.10, bf16[4,1024,128]{2,1,0:T(8,128)(2,1)} %get-tuple-element.492, bf16[256,128]{1,0:T(8,128)(2,1)} %copy-done.13, ...), kind=kOutput, calls=%fused_computation.17.clone.1 | convolution fusion | flops 339805952 | bytes 1412096 | tf_op jit(solution)/shard_map/while/body/eval_jaxpr/hnl,hnd->ld/dot_general | solution.py:52
  160.4 1.7 fusion.177
  162.1 1.5 fusion.178
  169.8 1.1 constant_dynamic-slice_fusion.19
  170.8 3.8 %fusion.170 = (f32[4,128]{1,0:T(4,128)S(1)}, f32[4,128,1536]{2,1,0:T(8,128)}) fusion(pred[128,1536]{1,0:T(8,128)(4,1)S(1)} %compare_select_fusion.4, bf16[4,1024,128]{2,1,0:T(8,128)(2,1)} %get-tuple-element.492, s32[]{:T(128)S(6)} %add.374, bf16[512,128]{1,0:T(8,128)(2,1)S(1)} %get-tuple-element.436, bf16[512,128]{1,0:T(8,128)(2,1)S(1)} %get-tuple-element.437, ...), kind=kOutput, calls=%fused_computation.133.clone.1 | convolution fusion | flops 205653504 | bytes 3868676 | tf_op jit(solution)/shard_map/while/body/eval_jaxpr/sub | solution.py:41
  175.8 2.6 fusion.171
  180.1 3.5 %fusion.174 = (f32[4,128]{1,0:T(4,128)S(1)}, f32[4,128,1280]{2,1,0:T(8,128)}) fusion(pred[128,1280]{1,0:T(8,128)(4,1)S(1)} %compare_select_fusion.5, bf16[4,1024,128]{2,1,0:T(8,128)(2,1)} %get-tuple-element.492, s32[]{:T(128)S(6)} %select_n.251, bf16[256,128]{1,0:T(8,128)(2,1)S(1)} %constant_dynamic-slice_fusion.21, ...), kind=kOutput, calls=%fused_computation.134.clone.1 | convolution fusion | flops 171377920 | bytes 3246084 | tf_op jit(solution)/shard_map/while/body/eval_jaxpr/sub | solution.py:41
  184.4 2.4 fusion.175
  186.8 1.1 copy-done.4
  189.2 2.9 convolution_bitcast_fusion.6
  192.1 3.5 %convolution_bitcast_fusion.7 = f32[1280,128]{1,0:T(8,128)} fusion(f32[4,128]{1,0:T(4,128)} %copy-done.17, bf16[4,1024,128]{2,1,0:T(8,128)(2,1)} %get-tuple-element.494, s32[]{:T(128)S(6)} %select_n.251, pred[128,1280]{1,0:T(8,128)(4,1)} %copy-done.10, bf16[4,1024,128]{2,1,0:T(8,128)(2,1)} %get-tuple-element.492, bf16[256,128]{1,0:T(8,128)(2,1)} %copy-done.13, ...), kind=kOutput, calls=%fused_computation.17.clone.1 | convolution fusion | flops 339805952 | bytes 1412096 | tf_op jit(solution)/shard_map/while/body/eval_jaxpr/hnl,hnd->ld/dot_general | solution.py:52
  195.6 1.7 fusion.177
  197.3 1.5 fusion.178
  204.9 1.1 constant_dynamic-slice_fusion.19
  206.0 3.8 %fusion.170 = (f32[4,128]{1,0:T(4,128)S(1)}, f32[4,128,1536]{2,1,0:T(8,128)}) fusion(pred[128,1536]{1,0:T(8,128)(4,1)S(1)} %compare_select_fusion.4, bf16[4,1024,128]{2,1,0:T(8,128)(2,1)} %get-tuple-element.492, s32[]{:T(128)S(6)} %add.374, bf16[512,128]{1,0:T(8,128)(2,1)S(1)} %get-tuple-element.436, bf16[512,128]{1,0:T(8,128)(2,1)S(1)} %get-tuple-element.437, ...), kind=kOutput, calls=%fused_computation.133.clone.1 | convolution fusion | flops 205653504 | bytes 3868676 | tf_op jit(solution)/shard_map/while/body/eval_jaxpr/sub | solution.py:41
  209.9 1.1 constant_dynamic-slice_fusion.20
  210.9 2.6 fusion.171
  215.3 3.5 %fusion.174 = (f32[4,128]{1,0:T(4,128)S(1)}, f32[4,128,1280]{2,1,0:T(8,128)}) fusion(pred[128,1280]{1,0:T(8,128)(4,1)S(1)} %compare_select_fusion.5, bf16[4,1024,128]{2,1,0:T(8,128)(2,1)} %get-tuple-element.492, s32[]{:T(128)S(6)} %select_n.251, bf16[256,128]{1,0:T(8,128)(2,1)S(1)} %constant_dynamic-slice_fusion.21, ...), kind=kOutput, calls=%fused_computation.134.clone.1 | convolution fusion | flops 171377920 | bytes 3246084 | tf_op jit(solution)/shard_map/while/body/eval_jaxpr/sub | solution.py:41
  219.6 2.4 fusion.175
  222.0 1.1 copy-done.4
  224.3 2.9 convolution_bitcast_fusion.6
  227.2 3.5 %convolution_bitcast_fusion.7 = f32[1280,128]{1,0:T(8,128)} fusion(f32[4,128]{1,0:T(4,128)} %copy-done.17, bf16[4,1024,128]{2,1,0:T(8,128)(2,1)} %get-tuple-element.494, s32[]{:T(128)S(6)} %select_n.251, pred[128,1280]{1,0:T(8,128)(4,1)} %copy-done.10, bf16[4,1024,128]{2,1,0:T(8,128)(2,1)} %get-tuple-element.492, bf16[256,128]{1,0:T(8,128)(2,1)} %copy-done.13, ...), kind=kOutput, calls=%fused_computation.17.clone.1 | convolution fusion | flops 339805952 | bytes 1412096 | tf_op jit(solution)/shard_map/while/body/eval_jaxpr/hnl,hnd->ld/dot_general | solution.py:52
  230.8 1.7 fusion.177
  232.5 1.5 fusion.178
  236.8 6.6 %all-to-all-start.3 = ((bf16[1,16,128,128]{3,2,0,1:T(8,128)(2,1)}), bf16[1,16,128,128]{3,2,0,1:T(8,128)(2,1)S(1)}, u32[]{:S(2)}, u32[]{:S(2)}) async-start(bf16[1,16,128,128]{3,2,0,1:T(8,128)(2,1)} %bitcast.37), calls=%async_computation.3 | async-start | bytes 1048576 | tf_op jit(solution)/shard_map/all_to_all | solution.py:222
  243.4 1.1 copy.52
  244.4 12.6 %all-to-all-done.3 = bf16[1,16,128,128]{3,2,0,1:T(8,128)(2,1)S(1)} async-done(((bf16[1,16,128,128]{3,2,0,1:T(8,128)(2,1)}), bf16[1,16,128,128]{3,2,0,1:T(8,128)(2,1)S(1)}, u32[]{:S(2)}, u32[]{:S(2)}) %all-to-all-start.3) | async-done | bytes 524320 | tf_op jit(solution)/shard_map/all_to_all | solution.py:222
  257.0 4.9 %all-to-all-start.2 = ((bf16[4,16,64,128]{3,2,0,1:T(8,128)(2,1)}), bf16[4,16,64,128]{3,2,0,1:T(8,128)(2,1)S(1)}, u32[]{:S(2)}, u32[]{:S(2)}) async-start(bf16[4,16,64,128]{3,2,0,1:T(8,128)(2,1)} %copy.52), calls=%async_computation.2 | async-start | bytes 2097152 | tf_op jit(solution)/shard_map/all_to_all | solution.py:221
  262.8 23.4 %all-to-all-done.2 = bf16[4,16,64,128]{3,2,0,1:T(8,128)(2,1)S(1)} async-done(((bf16[4,16,64,128]{3,2,0,1:T(8,128)(2,1)}), bf16[4,16,64,128]{3,2,0,1:T(8,128)(2,1)S(1)}, u32[]{:S(2)}, u32[]{:S(2)}) %all-to-all-start.2) | async-done | bytes 1048608 | tf_op jit(solution)/shard_map/all_to_all | solution.py:221
  286.2 5.6 %all-to-all-start.4 = ((bf16[1,16,128,128]{3,2,0,1:T(8,128)(2,1)}), bf16[1,16,128,128]{3,2,0,1:T(8,128)(2,1)S(1)}, u32[]{:S(2)}, u32[]{:S(2)}) async-start(bf16[1,16,128,128]{3,2,0,1:T(8,128)(2,1)} %bitcast.40), calls=%async_computation.4 | async-start | bytes 1048576 | tf_op jit(solution)/shard_map/all_to_all | solution.py:223
  291.8 1.1 copy.53
  292.8 1.3 collective-permute-start
  294.2 1.3 collective-permute-start.1
  295.5 9.9 %all-to-all-done.4 = bf16[1,16,128,128]{3,2,0,1:T(8,128)(2,1)S(1)} async-done(((bf16[1,16,128,128]{3,2,0,1:T(8,128)(2,1)}), bf16[1,16,128,128]{3,2,0,1:T(8,128)(2,1)S(1)}, u32[]{:S(2)}, u32[]{:S(2)}) %all-to-all-start.4) | async-done | bytes 524320 | tf_op jit(solution)/shard_map/all_to_all | solution.py:223
  305.5 1.3 collective-permute-start.2
  306.8 16.9 %collective-permute-done.1 = bf16[1,4,128,128]{3,2,1,0:T(8,128)(2,1)S(1)} collective-permute-done((bf16[1,4,128,128]{3,2,1,0:T(8,128)(2,1)S(1)}, bf16[1,4,128,128]{3,2,1,0:T(8,128)(2,1)S(1)}, u32[]{:S(2)}, u32[]{:S(2)}) %collective-permute-start.1) | collective-permute-done | bytes 131104 | tf_op jit(solution)/shard_map/ppermute | solution.py:15
  323.7 2.0 collective-permute-done.2
  (235 shorter events, 42.1 us)
Async XLA Ops:
  0.6 20.6 %copy-start = (s32[1,4,4,2]{2,3,1,0:T(2,128)S(1)}, s32[1,4,4,2]{2,3,1,0:T(2,128)}, u32[]{:S(2)}) copy-start(s32[1,4,4,2]{2,3,1,0:T(2,128)} %param.13) | copy-start | bytes 388
  0.6 10.6 %copy-start.8 = (bf16[1,32,128,128]{3,2,1,0:T(8,128)(2,1)S(1)}, bf16[1,32,128,128]{3,2,1,0:T(8,128)(2,1)}, u32[]{:S(2)}) copy-start(bf16[1,32,128,128]{3,2,1,0:T(8,128)(2,1)} %param.12) | copy-start | bytes 3145732
  0.7 10.7 %copy-start.14 = (bf16[1,32,128,128]{3,2,1,0:T(8,128)(2,1)S(1)}, bf16[1,32,128,128]{3,2,1,0:T(8,128)(2,1)}, u32[]{:S(2)}) copy-start(bf16[1,32,128,128]{3,2,1,0:T(8,128)(2,1)} %param.8) | copy-start | bytes 3145732
  3.0 8.5 %copy-start.15 = (bf16[1,4,128,128]{3,2,1,0:T(8,128)(2,1)S(1)}, bf16[1,4,128,128]{3,2,1,0:T(8,128)(2,1)}, u32[]{:S(2)}) copy-start(bf16[1,4,128,128]{3,2,1,0:T(8,128)(2,1)} %param.10) | copy-start | bytes 393220
  3.0 8.6 %copy-start.16 = (bf16[1,4,128,128]{3,2,1,0:T(8,128)(2,1)S(1)}, bf16[1,4,128,128]{3,2,1,0:T(8,128)(2,1)}, u32[]{:S(2)}) copy-start(bf16[1,4,128,128]{3,2,1,0:T(8,128)(2,1)} %param.9) | copy-start | bytes 393220
  5.0 11.2 %all-to-all-start.1 = ((bf16[16,2,128]{2,1,0:T(2,128)(2,1)}), bf16[16,2,128]{2,1,0:T(2,128)(2,1)S(1)}, u32[]{:S(2)}, u32[]{:S(2)}) async-start(bf16[16,2,128]{2,1,0:T(2,128)(2,1)} %reshape.286), calls=%async_computation.1 | async-start | bytes 16384 | tf_op jit(solution)/shard_map/all_to_all | solution.py:118
  16.2 73.4 %all-to-all-start = ((bf16[16,768,128]{2,1,0:T(8,128)(2,1)}), bf16[16,768,128]{2,1,0:T(8,128)(2,1)S(1)}, u32[]{:S(2)}, u32[]{:S(2)}) async-start(bf16[16,768,128]{2,1,0:T(8,128)(2,1)} %pad_maximum_fusion), calls=%async_computation | async-start | bytes 6291456 | tf_op jit(solution)/shard_map/all_to_all | solution.py:117
  98.0 6.3 %copy-start.7 = (pred[128,1536]{1,0:T(8,128)(4,1)}, pred[128,1536]{1,0:T(8,128)(4,1)S(1)}, u32[]{:S(2)}) copy-start(pred[128,1536]{1,0:T(8,128)(4,1)S(1)} %compare_select_fusion.4) | copy-start | bytes 589828 | tf_op jit(solution)/shard_map/while
  100.4 7.5 %copy-start.12 = (bf16[512,128]{1,0:T(8,128)(2,1)}, bf16[512,128]{1,0:T(8,128)(2,1)S(1)}, u32[]{:S(2)}) copy-start(bf16[512,128]{1,0:T(8,128)(2,1)S(1)} %get-tuple-element.436) | copy-start | bytes 393220 | tf_op jit(solution)/shard_map/while
  100.5 16.0 %copy-start.11 = (bf16[512,128]{1,0:T(8,128)(2,1)}, bf16[512,128]{1,0:T(8,128)(2,1)S(1)}, u32[]{:S(2)}) copy-start(bf16[512,128]{1,0:T(8,128)(2,1)S(1)} %get-tuple-element.437) | copy-start | bytes 393220 | tf_op jit(solution)/shard_map/while
  104.3 3.7 %copy-start.18 = (f32[4,128]{1,0:T(4,128)}, f32[4,128]{1,0:T(4,128)S(1)}, u32[]{:S(2)}) copy-start(f32[4,128]{1,0:T(4,128)S(1)} %get-tuple-element.440) | copy-start | bytes 6148 | tf_op jit(solution)/shard_map/while
  108.8 4.4 %copy-start.10 = (pred[128,1280]{1,0:T(8,128)(4,1)}, pred[128,1280]{1,0:T(8,128)(4,1)S(1)}, u32[]{:S(2)}) copy-start(pred[128,1280]{1,0:T(8,128)(4,1)S(1)} %compare_select_fusion.5) | copy-start | bytes 491524 | tf_op jit(solution)/shard_map/while
  109.7 6.7 %copy-start.13 = (bf16[256,128]{1,0:T(8,128)(2,1)}, bf16[256,128]{1,0:T(8,128)(2,1)S(1)}, u32[]{:S(2)}) copy-start(bf16[256,128]{1,0:T(8,128)(2,1)S(1)} %constant_dynamic-slice_fusion.21) | copy-start | bytes 196612 | tf_op jit(solution)/shard_map/while
  113.2 3.2 copy-start.17
  116.4 1.1 copy-start.4
  125.2 1.7 copy-start.5
  125.2 3.2 copy-start.1
  125.2 3.2 copy-start.6
  129.4 1.0 copy-start.2
  133.2 6.3 %copy-start.7 = (pred[128,1536]{1,0:T(8,128)(4,1)}, pred[128,1536]{1,0:T(8,128)(4,1)S(1)}, u32[]{:S(2)}) copy-start(pred[128,1536]{1,0:T(8,128)(4,1)S(1)} %compare_select_fusion.4) | copy-start | bytes 589828 | tf_op jit(solution)/shard_map/while
  135.6 7.5 %copy-start.12 = (bf16[512,128]{1,0:T(8,128)(2,1)}, bf16[512,128]{1,0:T(8,128)(2,1)S(1)}, u32[]{:S(2)}) copy-start(bf16[512,128]{1,0:T(8,128)(2,1)S(1)} %get-tuple-element.436) | copy-start | bytes 393220 | tf_op jit(solution)/shard_map/while
  135.7 15.9 %copy-start.11 = (bf16[512,128]{1,0:T(8,128)(2,1)}, bf16[512,128]{1,0:T(8,128)(2,1)S(1)}, u32[]{:S(2)}) copy-start(bf16[512,128]{1,0:T(8,128)(2,1)S(1)} %get-tuple-element.437) | copy-start | bytes 393220 | tf_op jit(solution)/shard_map/while
  139.5 3.6 %copy-start.18 = (f32[4,128]{1,0:T(4,128)}, f32[4,128]{1,0:T(4,128)S(1)}, u32[]{:S(2)}) copy-start(f32[4,128]{1,0:T(4,128)S(1)} %get-tuple-element.440) | copy-start | bytes 6148 | tf_op jit(solution)/shard_map/while
  144.0 4.4 %copy-start.10 = (pred[128,1280]{1,0:T(8,128)(4,1)}, pred[128,1280]{1,0:T(8,128)(4,1)S(1)}, u32[]{:S(2)}) copy-start(pred[128,1280]{1,0:T(8,128)(4,1)S(1)} %compare_select_fusion.5) | copy-start | bytes 491524 | tf_op jit(solution)/shard_map/while
  144.9 6.7 %copy-start.13 = (bf16[256,128]{1,0:T(8,128)(2,1)}, bf16[256,128]{1,0:T(8,128)(2,1)S(1)}, u32[]{:S(2)}) copy-start(bf16[256,128]{1,0:T(8,128)(2,1)S(1)} %constant_dynamic-slice_fusion.21) | copy-start | bytes 196612 | tf_op jit(solution)/shard_map/while
  148.4 3.2 copy-start.17
  151.6 1.1 copy-start.4
  160.4 1.7 copy-start.5
  160.4 3.2 copy-start.1
  160.4 3.2 copy-start.6
  164.6 1.0 copy-start.2
  168.4 6.3 %copy-start.7 = (pred[128,1536]{1,0:T(8,128)(4,1)}, pred[128,1536]{1,0:T(8,128)(4,1)S(1)}, u32[]{:S(2)}) copy-start(pred[128,1536]{1,0:T(8,128)(4,1)S(1)} %compare_select_fusion.4) | copy-start | bytes 589828 | tf_op jit(solution)/shard_map/while
  170.8 7.5 %copy-start.12 = (bf16[512,128]{1,0:T(8,128)(2,1)}, bf16[512,128]{1,0:T(8,128)(2,1)S(1)}, u32[]{:S(2)}) copy-start(bf16[512,128]{1,0:T(8,128)(2,1)S(1)} %get-tuple-element.436) | copy-start | bytes 393220 | tf_op jit(solution)/shard_map/while
  170.8 15.9 %copy-start.11 = (bf16[512,128]{1,0:T(8,128)(2,1)}, bf16[512,128]{1,0:T(8,128)(2,1)S(1)}, u32[]{:S(2)}) copy-start(bf16[512,128]{1,0:T(8,128)(2,1)S(1)} %get-tuple-element.437) | copy-start | bytes 393220 | tf_op jit(solution)/shard_map/while
  174.7 3.6 %copy-start.18 = (f32[4,128]{1,0:T(4,128)}, f32[4,128]{1,0:T(4,128)S(1)}, u32[]{:S(2)}) copy-start(f32[4,128]{1,0:T(4,128)S(1)} %get-tuple-element.440) | copy-start | bytes 6148 | tf_op jit(solution)/shard_map/while
  179.2 4.4 %copy-start.10 = (pred[128,1280]{1,0:T(8,128)(4,1)}, pred[128,1280]{1,0:T(8,128)(4,1)S(1)}, u32[]{:S(2)}) copy-start(pred[128,1280]{1,0:T(8,128)(4,1)S(1)} %compare_select_fusion.5) | copy-start | bytes 491524 | tf_op jit(solution)/shard_map/while
  180.1 6.7 %copy-start.13 = (bf16[256,128]{1,0:T(8,128)(2,1)}, bf16[256,128]{1,0:T(8,128)(2,1)S(1)}, u32[]{:S(2)}) copy-start(bf16[256,128]{1,0:T(8,128)(2,1)S(1)} %constant_dynamic-slice_fusion.21) | copy-start | bytes 196612 | tf_op jit(solution)/shard_map/while
  183.6 3.2 copy-start.17
  186.8 1.1 copy-start.4
  195.6 1.7 copy-start.5
  195.6 3.2 copy-start.1
  195.6 3.2 copy-start.6
  199.8 1.0 copy-start.2
  203.6 6.3 %copy-start.7 = (pred[128,1536]{1,0:T(8,128)(4,1)}, pred[128,1536]{1,0:T(8,128)(4,1)S(1)}, u32[]{:S(2)}) copy-start(pred[128,1536]{1,0:T(8,128)(4,1)S(1)} %compare_select_fusion.4) | copy-start | bytes 589828 | tf_op jit(solution)/shard_map/while
  206.0 7.5 %copy-start.12 = (bf16[512,128]{1,0:T(8,128)(2,1)}, bf16[512,128]{1,0:T(8,128)(2,1)S(1)}, u32[]{:S(2)}) copy-start(bf16[512,128]{1,0:T(8,128)(2,1)S(1)} %get-tuple-element.436) | copy-start | bytes 393220 | tf_op jit(solution)/shard_map/while
  206.0 15.9 %copy-start.11 = (bf16[512,128]{1,0:T(8,128)(2,1)}, bf16[512,128]{1,0:T(8,128)(2,1)S(1)}, u32[]{:S(2)}) copy-start(bf16[512,128]{1,0:T(8,128)(2,1)S(1)} %get-tuple-element.437) | copy-start | bytes 393220 | tf_op jit(solution)/shard_map/while
  209.9 3.6 %copy-start.18 = (f32[4,128]{1,0:T(4,128)}, f32[4,128]{1,0:T(4,128)S(1)}, u32[]{:S(2)}) copy-start(f32[4,128]{1,0:T(4,128)S(1)} %get-tuple-element.440) | copy-start | bytes 6148 | tf_op jit(solution)/shard_map/while
  214.3 4.4 %copy-start.10 = (pred[128,1280]{1,0:T(8,128)(4,1)}, pred[128,1280]{1,0:T(8,128)(4,1)S(1)}, u32[]{:S(2)}) copy-start(pred[128,1280]{1,0:T(8,128)(4,1)S(1)} %compare_select_fusion.5) | copy-start | bytes 491524 | tf_op jit(solution)/shard_map/while
  215.3 6.7 %copy-start.13 = (bf16[256,128]{1,0:T(8,128)(2,1)}, bf16[256,128]{1,0:T(8,128)(2,1)S(1)}, u32[]{:S(2)}) copy-start(bf16[256,128]{1,0:T(8,128)(2,1)S(1)} %constant_dynamic-slice_fusion.21) | copy-start | bytes 196612 | tf_op jit(solution)/shard_map/while
  218.7 3.2 copy-start.17
  222.0 1.1 copy-start.4
  230.8 1.7 copy-start.5
  230.8 3.2 copy-start.1
  230.8 3.2 copy-start.6
  234.0 0.9 slice-start
  234.9 1.0 copy-start.2
  235.9 7.4 %copy-start.9 = (bf16[4,1024,128]{2,1,0:T(8,128)(2,1)S(1)}, bf16[4,1024,128]{2,1,0:T(8,128)(2,1)}, u32[]{:S(2)}) copy-start(bf16[4,1024,128]{2,1,0:T(8,128)(2,1)} %get-tuple-element.300) | copy-start | bytes 3145732
  236.8 25.2 %copy-start.3 = (f32[2048,128]{1,0:T(8,128)S(1)}, f32[2048,128]{1,0:T(8,128)}, u32[]{:S(2)}) copy-start(f32[2048,128]{1,0:T(8,128)} %get-tuple-element.302) | copy-start | bytes 3145732
  236.8 20.2 %all-to-all-start.3 = ((bf16[1,16,128,128]{3,2,0,1:T(8,128)(2,1)}), bf16[1,16,128,128]{3,2,0,1:T(8,128)(2,1)S(1)}, u32[]{:S(2)}, u32[]{:S(2)}) async-start(bf16[1,16,128,128]{3,2,0,1:T(8,128)(2,1)} %bitcast.37), calls=%async_computation.3 | async-start | bytes 1048576 | tf_op jit(solution)/shard_map/all_to_all | solution.py:222
  257.0 29.2 %all-to-all-start.2 = ((bf16[4,16,64,128]{3,2,0,1:T(8,128)(2,1)}), bf16[4,16,64,128]{3,2,0,1:T(8,128)(2,1)S(1)}, u32[]{:S(2)}, u32[]{:S(2)}) async-start(bf16[4,16,64,128]{3,2,0,1:T(8,128)(2,1)} %copy.52), calls=%async_computation.2 | async-start | bytes 2097152 | tf_op jit(solution)/shard_map/all_to_all | solution.py:221
  286.2 19.2 %all-to-all-start.4 = ((bf16[1,16,128,128]{3,2,0,1:T(8,128)(2,1)}), bf16[1,16,128,128]{3,2,0,1:T(8,128)(2,1)S(1)}, u32[]{:S(2)}, u32[]{:S(2)}) async-start(bf16[1,16,128,128]{3,2,0,1:T(8,128)(2,1)} %bitcast.40), calls=%async_computation.4 | async-start | bytes 1048576 | tf_op jit(solution)/shard_map/all_to_all | solution.py:223
  292.8 32.9 %collective-permute-start = (bf16[1,32,128,128]{3,2,1,0:T(8,128)(2,1)}, bf16[1,32,128,128]{3,2,1,0:T(8,128)(2,1)S(1)}, u32[]{:S(2)}, u32[]{:S(2)}) collective-permute-start(bf16[1,32,128,128]{3,2,1,0:T(8,128)(2,1)} %bitcast.36), channel_id=1, source_target_pairs={{1,0},{3,2},{5,4},{7,6},{9,8},{11,10},{13,12},{15,14},{17,16},{19,... | collective-permute-start | bytes 3145736 | tf_op jit(solution)/shard_map/ppermute | solution.py:15
  294.2 29.5 %collective-permute-start.1 = (bf16[1,4,128,128]{3,2,1,0:T(8,128)(2,1)S(1)}, bf16[1,4,128,128]{3,2,1,0:T(8,128)(2,1)S(1)}, u32[]{:S(2)}, u32[]{:S(2)}) collective-permute-start(bf16[1,4,128,128]{3,2,1,0:T(8,128)(2,1)S(1)} %bitcast.139), channel_id=1, source_target_pairs={{1,0},{3,2},{5,4},{7,6},{9,8},{11,10},{13,12},{15,14},{17,16},{19,... | collective-permute-start | bytes 393224 | tf_op jit(solution)/shard_map/ppermute | solution.py:15
  305.5 20.3 %collective-permute-start.2 = (bf16[1,4,128,128]{3,2,1,0:T(8,128)(2,1)S(1)}, bf16[1,4,128,128]{3,2,1,0:T(8,128)(2,1)S(1)}, u32[]{:S(2)}, u32[]{:S(2)}) collective-permute-start(bf16[1,4,128,128]{3,2,1,0:T(8,128)(2,1)S(1)} %bitcast.140), channel_id=1, source_target_pairs={{1,0},{3,2},{5,4},{7,6},{9,8},{11,10},{13,12},{15,14},{17,16},{19,... | collective-permute-start | bytes 393224 | tf_op jit(solution)/shard_map/ppermute | solution.py:15
  (3 other events, 2.7 us)
where the time goes:
time: 332 us; the launch traced here: 328 us
  waiting for transfers between devices  135 us (41%)
  matrix products  91.6 us (28%)
  local copies, waits for them, and re-layouts  43.6 us (13%)
  starting transfers between devices  32.3 us (10%)
  other arithmetic  13.2 us (4%)
  loops' own time  11.5 us (3%)
    all_to_all x1, waiting for transfers between devices, on_device(): lax.all_to_all(packed, 'seq', split_axis=0, concat_axis=1, tiled=True)  67.3 us
    sub x8, matrix products, attend_rows(): weights_raw = jnp.exp(scores - row_max)  29.3 us
    dot_general x8, matrix products, attend_rows(): jnp.einsum('hnl,hnd->ld', probs_low, grad_rows, preferred_element_type=jn...  25.8 us
    all_to_all x1, waiting for transfers between devices, on_device(): lax.all_to_all(query_out_send, 'seq', split_axis=1, concat_axis=0, tiled=...  23.4 us
    dot_general x8, matrix products, attend_rows(): jnp.einsum('hnd,ld->hnl', grad_rows, value_rows, preferred_element_type=j...  19.7 us
    ppermute x3, waiting for transfers between devices, shifted(): return lax.ppermute(block, axis, route)  19 us
    all_to_all x1, waiting for transfers between devices, on_device(): lax.all_to_all(key_out_send, 'seq', split_axis=1, concat_axis=0, tiled=True)  12.6 us
    dot_general x8, matrix products, attend_rows(): jnp.einsum('hnl,hnd->ld', dscores, query_rows, preferred_element_type=jnp...  12.5 us
  transfers between devices with their start and end apart: 8, of which 7 were waited for; matrix products, arithmetic and copies ran while one was open for 2% of the time, Pallas kernels for 0%

commit v1 on v0

v1 whole, which is shorter than its diff:
```python
import functools
import math

import jax
import jax.numpy as jnp
from jax import lax
from jax.experimental import pallas as pl
from jax.experimental.pallas import tpu as pltpu
from jax.sharding import PartitionSpec as P

BLK = 512
TILE_HEADS = 2
FAR = 1e30


def nt(a, b):
    return lax.dot_general(a, b, (((1,), (1,)), ((), ())), preferred_element_type=jnp.float32)


def nn(a, b):
    return lax.dot_general(a, b, (((1,), (0,)), ((), ())), preferred_element_type=jnp.float32)


def tn(a, b):
    return lax.dot_general(a, b, (((0,), (0,)), ((), ())), preferred_element_type=jnp.float32)


def attend_kernel(sizes, meta, *refs):
    members, reach, heads, rows, feature = sizes
    take = list(refs)
    queries, grads, deltas = take[:3]
    packs = take[3 : 2 + members]
    take = take[2 + members :]
    near, far = take[0], take[1 : 1 + reach]
    take = take[1 + reach :]
    query_outs, take = take[:members], take[members:]
    far_outs, take = take[:reach], take[reach:]
    (own_out, query_buf, grad_buf, low_buf, delta_buf, pair_buf, key_acc, value_acc, query_done,
     far_done, own_done, blank, in_sem, pair_sem, out_sem) = take
    mine = meta[0]
    offsets = (meta[1], meta[2])
    height = heads * rows
    lanes = TILE_HEADS * rows
    factor = feature ** (-0.5)
    sharp = factor * math.log2(math.e)

    own_copies = []
    for hop in range(members):
        spot = mine ^ hop
        copy = pltpu.make_async_copy(near.at[:, hop], pair_buf.at[2, :, spot], pair_sem.at[2])
        copy.start()
        own_copies.append(copy)
    for slot in range(2):
        for hop in range(reach + 1):
            source = near if hop == 0 else far[hop - 1]

            @pl.when(offsets[slot] == hop)
            def _(source=source, slot=slot):
                pltpu.make_async_copy(source, pair_buf.at[slot], pair_sem.at[slot]).start()

    first = pl.ds(mine * heads, heads)
    piece_copies = []
    for hop in range(members):
        spot = mine ^ hop
        if hop == 0:
            parts = (
                (queries.at[0, first], query_buf.at[spot]),
                (grads.at[0, first], grad_buf.at[spot]),
                (deltas.at[mine], low_buf.at[spot]),
            )
        else:
            pack = packs[hop - 1]
            parts = (
                (pack.at[pl.ds(0, heads)], query_buf.at[spot]),
                (pack.at[pl.ds(heads, heads)], grad_buf.at[spot]),
                (pack.at[2 * heads, pl.ds(0, 16)], low_buf.at[spot]),
            )
        for source, target in parts:
            copy = pltpu.make_async_copy(source, target, in_sem.at[hop])
            copy.start()
            piece_copies.append(copy)
    key_acc[...] = jnp.zeros_like(key_acc)
    value_acc[...] = jnp.zeros_like(value_acc)
    blank[...] = jnp.zeros_like(blank)
    for copy in own_copies:
        copy.wait()
    for slot in range(2):
        pltpu.make_async_copy(near, pair_buf.at[slot], pair_sem.at[slot]).wait()
    for copy in piece_copies:
        copy.wait()
    delta_buf[...] = low_buf[...].astype(jnp.float32)

    biases = [jnp.where(offset > 0, 0.0, FAR) for offset in offsets]
    key_ids = lax.broadcasted_iota(jnp.int32, (rows, lanes), 0)
    row_ids = lax.broadcasted_iota(jnp.int32, (rows, lanes), 1) % rows
    causal = key_ids <= row_ids

    for spot in range(members):
        visible = (spot + 1) * rows

        def tile(step, carry, spot=spot, visible=visible):
            here = pl.ds(step * TILE_HEADS, TILE_HEADS)
            query = query_buf[spot, here].reshape(lanes, feature)
            grad = grad_buf[spot, here].reshape(lanes, feature)
            delta = jnp.concatenate(
                [
                    delta_buf[spot, pl.ds(step * TILE_HEADS + i, 1), :]
                    for i in range(TILE_HEADS)
                ],
                axis=1,
            )
            spans = [(0, BLK), (1, BLK), (2, visible)]

            def fetch(part, slot, length):
                return pair_buf[slot, part].reshape(members * rows, feature)[:length]

            scores = [nt(fetch(0, slot, length), query) for slot, length in spans]
            edge = jnp.where(causal, scores[2][visible - rows :], -FAR)
            scores[2] = (
                edge
                if spot == 0
                else jnp.concatenate([scores[2][: visible - rows], edge], axis=0)
            )
            tops = [jnp.max(score, axis=0, keepdims=True) for score in scores]
            top = jnp.maximum(jnp.maximum(tops[0] - biases[0], tops[1] - biases[1]), tops[2])
            shifts = [top + biases[0], top + biases[1], top]
            raws = [jnp.exp2((score - shift) * sharp) for score, shift in zip(scores, shifts)]
            total = sum(jnp.sum(raw, axis=0, keepdims=True) for raw in raws)
            inverse = 1.0 / total
            query_sum = jnp.zeros((lanes, feature), jnp.float32)
            for (slot, length), raw in zip(spans, raws):
                dprobs = nt(fetch(1, slot, length), grad)
                probs = raw * inverse
                dscores = (probs * (dprobs - delta)).astype(jnp.bfloat16)
                base = slot * BLK
                value_acc[base : base + length] += nn(probs.astype(jnp.bfloat16), grad)
                key_acc[base : base + length] += nn(dscores, query)
                query_sum += tn(dscores, fetch(0, slot, length))
            query_done[spot, here] = (
                (query_sum * factor).astype(jnp.bfloat16).reshape(TILE_HEADS, rows, feature)
            )
            return carry

        lax.fori_loop(0, heads // TILE_HEADS, tile, 0)

    shape = (members, rows, feature)
    for slot in range(2):
        span = slice(slot * BLK, (slot + 1) * BLK)
        far_done[slot, 0] = (key_acc[span] * factor).astype(jnp.bfloat16).reshape(shape)
        far_done[slot, 1] = value_acc[span].astype(jnp.bfloat16).reshape(shape)
    own_done[0] = (key_acc[2 * BLK :] * factor).reshape(shape)
    own_done[1] = value_acc[2 * BLK :].reshape(shape)

    final = []
    for hop in range(1, reach + 1):
        target = far_outs[hop - 1]
        for slot in range(2):

            @pl.when(offsets[slot] == hop)
            def _(target=target, slot=slot):
                pltpu.make_async_copy(far_done.at[slot], target, out_sem.at[hop]).start()

        @pl.when((offsets[0] != hop) & (offsets[1] != hop))
        def _(target=target):
            pltpu.make_async_copy(blank, target, out_sem.at[hop]).start()

        final.append(pltpu.make_async_copy(blank, target, out_sem.at[hop]))
    for hop in range(members):
        spot = mine ^ hop
        for source, target in (
            (own_done.at[:, spot], own_out.at[:, hop]),
            (query_done.at[spot], query_outs[hop]),
        ):
            copy = pltpu.make_async_copy(source, target, out_sem.at[0])
            copy.start()
            final.append(copy)
    for copy in final:
        copy.wait()


def attend(meta, queries, grads, deltas, packs, near, far, sizes):
    members, reach, heads, rows, feature = sizes
    low, wide = jnp.bfloat16, jnp.float32
    pair = (2, members, rows, feature)
    anywhere = pl.BlockSpec(memory_space=pl.ANY)
    outs = (
        [jax.ShapeDtypeStruct((heads, rows, feature), low)] * members
        + [jax.ShapeDtypeStruct(pair, low)] * reach
        + [jax.ShapeDtypeStruct(pair, wide)]
    )
    results = pl.pallas_call(
        functools.partial(attend_kernel, sizes),
        out_shape=outs,
        in_specs=[pl.BlockSpec(memory_space=pltpu.SMEM)]
        + [anywhere] * (3 + len(packs) + 1 + reach),
        out_specs=[anywhere] * len(outs),
        scratch_shapes=[
            pltpu.VMEM((members, heads, rows, feature), low),
            pltpu.VMEM((members, heads, rows, feature), low),
            pltpu.VMEM((members, 16, rows), low),
            pltpu.VMEM((members, 16, rows), wide),
            pltpu.VMEM((3,) + pair, low),
            pltpu.VMEM((3 * BLK, feature), wide),
            pltpu.VMEM((3 * BLK, feature), wide),
            pltpu.VMEM((members, heads, rows, feature), low),
            pltpu.VMEM((2,) + pair, low),
            pltpu.VMEM(pair, wide),
            pltpu.VMEM(pair, low),
            pltpu.SemaphoreType.DMA((members,)),
            pltpu.SemaphoreType.DMA((3,)),
            pltpu.SemaphoreType.DMA((reach + 1,)),
        ],
        compiler_params=pltpu.CompilerParams(vmem_limit_bytes=48 * 1024 * 1024),
    )(meta, queries, grads, deltas, *packs, near, *far)
    return (
        results[:members],
        results[members : members + reach],
        results[members + reach],
    )


def settle_kernel(members, heads, meta, *refs):
    query_parts, pair_parts = refs[:members], refs[members : 2 * members]
    query_out, key_out, value_out, sem = refs[2 * members :]
    mine = meta[0]
    copies = []
    for hop in range(members):
        owner = mine ^ hop
        for source, target in (
            (query_parts[hop], query_out.at[0, pl.ds(owner * heads, heads)]),
            (pair_parts[hop].at[0], key_out.at[0, owner]),
            (pair_parts[hop].at[1], value_out.at[0, owner]),
        ):
            copy = pltpu.make_async_copy(source, target, sem)
            copy.start()
            copies.append(copy)
    for copy in copies:
        copy.wait()


def settle(meta, query_parts, pair_parts, shapes):
    members = len(query_parts)
    heads = query_parts[0].shape[0]
    anywhere = pl.BlockSpec(memory_space=pl.ANY)
    return pl.pallas_call(
        functools.partial(settle_kernel, members, heads),
        out_shape=[jax.ShapeDtypeStruct(shape, jnp.bfloat16) for shape in shapes],
        in_specs=[pl.BlockSpec(memory_space=pltpu.SMEM)] + [anywhere] * (2 * members),
        out_specs=[anywhere] * 3,
        scratch_shapes=[pltpu.SemaphoreType.DMA],
    )(meta, *query_parts, *pair_parts)


def on_device(queries, key_states, value_states, outputs, out_grads, selected):
    devices = lax.axis_size("seq")
    sections = lax.axis_size("pipe")
    head_count, rows, feature = queries.shape[1:]
    key_heads = key_states.shape[1]
    members = BLK // rows
    heads = head_count // key_heads
    reach = devices // members - 1
    assert members == key_heads and members & (members - 1) == 0 and heads <= 16
    rank = lax.axis_index("seq")
    mine = rank % members
    block = rank // members

    def around(tensor, hop):
        return lax.ppermute(tensor, "seq", [(i, i ^ hop) for i in range(devices)])

    def along(tensor, hop):
        step = members * hop
        route = [(i, i + step) for i in range(devices) if 0 <= i + step < devices]
        return lax.ppermute(tensor, "seq", route)

    def previous(tensor, hop):
        route = [
            (i * sections + s, (i ^ hop) * sections + s - 1)
            for i in range(devices)
            for s in range(1, sections)
        ]
        return lax.ppermute(tensor, ("seq", "pipe"), route)

    chosen = lax.dynamic_slice(selected, (0, block, mine, 0), (1, 1, 1, 2)).reshape(2)
    usable = chosen < block
    offsets = jnp.where(usable, block - chosen, 0)
    meta = jnp.concatenate([mine[None], offsets]).astype(jnp.int32)

    pairs = jnp.stack([key_states[0], value_states[0]], axis=0)

    def pair_of(hop):
        return lax.dynamic_index_in_dim(pairs, mine ^ hop, axis=1, keepdims=False)

    pieces = [pair_of(0)] + [around(pair_of(hop), hop) for hop in range(1, members)]
    near = jnp.stack(pieces, axis=1)
    far = [along(near, hop) for hop in range(1, reach + 1)]

    deltas = jnp.sum(
        out_grads[0].astype(jnp.float32) * outputs[0].astype(jnp.float32), axis=-1
    ).astype(jnp.bfloat16)
    deltas = deltas.reshape(key_heads, heads, rows)
    deltas = jnp.pad(deltas, ((0, 0), (0, 16 - heads), (0, 0)))

    packs = []
    for hop in range(1, members):
        other = mine ^ hop
        query_part = lax.dynamic_slice_in_dim(queries[0], other * heads, heads, 0)
        grad_part = lax.dynamic_slice_in_dim(out_grads[0], other * heads, heads, 0)
        delta_part = lax.dynamic_index_in_dim(deltas, other, axis=0, keepdims=True)
        delta_part = jnp.pad(delta_part, ((0, 0), (0, rows - 16), (0, 0)))
        packs.append(around(jnp.concatenate([query_part, grad_part, delta_part], axis=0), hop))

    sizes = (members, reach, heads, rows, feature)
    query_parts, far_parts, own_part = attend(
        meta, queries, out_grads, deltas, packs, near, far, sizes
    )
    query_back = [previous(part, hop) for hop, part in enumerate(query_parts)]
    summed = own_part
    for hop in range(1, reach + 1):
        summed = summed + along(far_parts[hop - 1], -hop).astype(jnp.float32)
    summed = summed.astype(jnp.bfloat16)
    pair_back = [previous(summed[:, hop], hop) for hop in range(members)]
    shapes = (queries.shape, key_states.shape, value_states.shape)
    return tuple(settle(meta, query_back, pair_back, shapes))


def solution(mesh):
    return jax.shard_map(
        on_device,
        mesh=mesh,
        in_specs=(
            P("pipe", None, "seq", None),
            P("pipe", None, "seq", None),
            P("pipe", None, "seq", None),
            P("pipe", None, "seq", None),
            P("pipe", None, "seq", None),
            P("pipe", None, None, None),
        ),
        out_specs=(
            P("pipe", None, "seq", None),
            P("pipe", None, "seq", None),
            P("pipe", None, "seq", None),
        ),
        check_vma=False,
    )
```

time: 332 us -> 153 us (0.46)
  the two profiles are of different devices: /device:TPU:8 before, /device:TPU:16 now
where the time goes in v1:
time: 153 us; the launch traced here: 152 us
  Pallas kernels  70 us (46%)
  waiting for transfers between devices  38.4 us (25%)
  starting transfers between devices  34.3 us (22%)
  other arithmetic  5.68 us (4%)
  local copies, waits for them, and re-layouts  2.81 us (2%)
    pallas_call x1, Pallas kernels, settle(): pl.pallas_call(functools.partial(settle_kernel, members, heads), out_shap...  41.5 us
    pallas_call x1, Pallas kernels, attend(): pl.pallas_call(functools.partial(attend_kernel, sizes), out_shape=outs, i...  28.5 us
    ppermute x6, waiting for transfers between devices, along(): return lax.ppermute(tensor, 'seq', route)  25.2 us
    ppermute x6, starting transfers between devices, along(): return lax.ppermute(tensor, 'seq', route)  20.2 us
    ppermute x8, waiting for transfers between devices, previous(): return lax.ppermute(tensor, ('seq', 'pipe'), route)  13.2 us
    ppermute x8, starting transfers between devices, previous(): return lax.ppermute(tensor, ('seq', 'pipe'), route)  10.3 us
    ppermute x6, starting transfers between devices, around(): return lax.ppermute(tensor, 'seq', [(i, i ^ hop) for i in range(devices)])  3.79 us
  transfers between devices with their start and end apart: 20, of which 7 were waited for; matrix products, arithmetic and copies ran while one was open for 4% of the time, Pallas kernels for 0%

profile of v1, /device:TPU:16, one launch (start us, length us, event | category | flops | bytes accessed | tf_op | source)
XLA Modules:
  0.0 152.4 jit_solution(1529070754575749037)
XLA Ops:
  0.6 0.0 copy-start.2
  0.7 1.0 constant_dynamic-update-slice_fusion.1
  1.7 0.9 constant_dynamic-update-slice_fusion
  2.7 1.0 collective-permute-start.5
  3.7 0.6 collective-permute-start.4
  4.3 0.3 collective-permute-start.3
  4.6 0.0 copy-done.2
  4.6 1.9 %multiply_reduce_fusion = bf16[32,128]{1,0:T(8,128)(2,1)S(1)} fusion(bf16[1,32,128,128]{3,2,1,0:T(8,128)(2,1)} %param.9, bf16[1,32,128,128]{3,2,1,0:T(8,128)(2,1)S(1)} %copy-done.2), kind=kLoop, calls=%fused_computation | loop fusion | flops 2093056 | bytes 2105344 | tf_op jit(solution)/shard_map/reduce_sum | solution.py:297
  6.6 0.0 copy-done
  6.6 0.1 dynamic-slice_bitcast_fusion
  6.7 0.9 fusion.3
  7.6 0.2 collective-permute-start
  7.8 0.9 fusion.4
  8.7 1.4 collective-permute-start.1
  10.1 0.9 fusion.5
  10.9 0.0 collective-permute-done.5
  10.9 0.3 collective-permute-start.2
  11.2 0.0 collective-permute-done.4
  11.2 0.0 collective-permute-done.3
  11.2 0.7 collective-permute-start.8
  11.9 1.3 collective-permute-start.7
  13.2 0.0 collective-permute-done.8.refs_9_
  13.2 14.4 %collective-permute-start.6 = (bf16[2,4,128,128]{3,2,1,0:T(8,128)(2,1)S(1)}, bf16[2,4,128,128]{3,2,1,0:T(8,128)(2,1)}, u32[]{:S(2)}, u32[]{:S(2)}) collective-permute-start(bf16[2,4,128,128]{3,2,1,0:T(8,128)(2,1)S(1)} %pad_maximum_fusion.refs_6_), channel_id=1, source_target_pairs={{0,8},{2,10},{4,12},{6,14},{8,16},{10,18},{12,20},{14,22},{16,24},... | collective-permute-start | bytes 786440 | tf_op jit(solution)/shard_map/ppermute | solution.py:273
  27.7 0.9 fusion.9
  28.5 0.1 pad_add_fusion.meta
  28.6 1.2 collective-permute-done.7.refs_8_
  29.8 10.9 %collective-permute-done.6.refs_7_ = bf16[2,4,128,128]{3,2,1,0:T(8,128)(2,1)} collective-permute-done((bf16[2,4,128,128]{3,2,1,0:T(8,128)(2,1)S(1)}, bf16[2,4,128,128]{3,2,1,0:T(8,128)(2,1)}, u32[]{:S(2)}, u32[]{:S(2)}) %collective-permute-start.6) | collective-permute-done | bytes 262176 | tf_op jit(solution)/shard_map/ppermute | solution.py:273
  40.8 0.0 collective-permute-done.refs_3_
  40.8 0.0 collective-permute-done.1.refs_4_
  40.8 0.0 collective-permute-done.2.refs_5_
  40.8 28.5 %shard_map.85 = (bf16[8,128,128]{2,1,0:T(8,128)(2,1)S(1)}, bf16[8,128,128]{2,1,0:T(8,128)(2,1)S(1)}, bf16[8,128,128]{2,1,0:T(8,128)(2,1)S(1)}, bf16[8,128,128]{2...) custom-call(s32[3]{0:T(128)S(1)} %pad_add_fusion.meta, ...), custom_call_target="tpu_custom_call" | custom-call | tf_op jit(solution)/shard_map/pallas_call | solution.py:191
  69.3 0.0 copy-done.1
  69.3 0.7 collective-permute-start.15
  70.0 1.3 collective-permute-start.14
  71.4 1.9 %collective-permute-start.13 = (bf16[2,4,128,128]{3,2,0,1:T(8,128)(2,1)S(1)}, bf16[2,4,128,128]{3,2,0,1:T(8,128)(2,1)S(1)}, u32[]{:S(2)}, u32[]{:S(2)}) collective-permute-start(bf16[2,4,128,128]{3,2,0,1:T(8,128)(2,1)S(1)} %copy.9), channel_id=1, source_target_pairs={{8,0},{10,2},{12,4},{14,6},{16,8},{18,10},{20,12},{22,14},{24,16},... | collective-permute-start | bytes 786440 | tf_op jit(solution)/shard_map/ppermute | solution.py:273
  73.3 1.3 collective-permute-start.9
  74.6 1.3 collective-permute-start.10
  75.9 0.0 collective-permute-done.15
  75.9 1.3 collective-permute-start.11
  77.2 8.7 %collective-permute-done.14 = bf16[2,4,128,128]{3,2,0,1:T(8,128)(2,1)S(1)} collective-permute-done((bf16[2,4,128,128]{3,2,0,1:T(8,128)(2,1)S(1)}, bf16[2,4,128,128]{3,2,0,1:T(8,128)(2,1)S(1)}, u32[]{:S(2)}, u32[]{:S(2)}) %collective-permute-start.14) | collective-permute-done | bytes 262176 | tf_op jit(solution)/shard_map/ppermute | solution.py:273
  85.9 1.3 collective-permute-start.12
  87.2 4.3 %collective-permute-done.13 = bf16[2,4,128,128]{3,2,0,1:T(8,128)(2,1)S(1)} collective-permute-done((bf16[2,4,128,128]{3,2,0,1:T(8,128)(2,1)S(1)}, bf16[2,4,128,128]{3,2,0,1:T(8,128)(2,1)S(1)}, u32[]{:S(2)}, u32[]{:S(2)}) %collective-permute-start.13) | collective-permute-done | bytes 262176 | tf_op jit(solution)/shard_map/ppermute | solution.py:273
  91.5 0.1 fusion.8
  91.7 1.3 collective-permute-start.19
  93.0 0.0 collective-permute-done.9.refs_0_
  93.0 0.0 copy-start.3
  93.0 1.3 collective-permute-start.18
  94.3 8.0 %collective-permute-done.10.refs_1_ = bf16[8,128,128]{2,1,0:T(8,128)(2,1)S(1)} collective-permute-done((bf16[8,128,128]{2,1,0:T(8,128)(2,1)S(1)}, bf16[8,128,128]{2,1,0:T(8,128)(2,1)S(1)}, u32[]{:S(2)}, u32[]{:S(2)}) %collective-permute-start.10) | collective-permute-done | bytes 262176 | tf_op jit(solution)/shard_map/ppermute | solution.py:281
  102.3 1.3 collective-permute-start.17
  103.6 0.0 collective-permute-done.11.refs_2_
  103.6 0.0 copy-start.5
  103.7 1.3 collective-permute-start.16
  105.0 0.0 collective-permute-done.12.refs_3_
  105.0 0.0 copy-start.6
  105.0 0.0 collective-permute-done.19.refs_7_
  105.0 0.0 copy-start.7
  105.0 0.0 collective-permute-done.18.refs_6_
  105.0 0.0 copy-start.8
  105.0 2.9 %collective-permute-done.17.refs_5_ = bf16[2,128,128]{2,1,0:T(8,128)(2,1)S(1)} collective-permute-done((bf16[2,128,128]{2,1,0:T(8,128)(2,1)S(1)}, bf16[2,128,128]{2,1,0:T(8,128)(2,1)S(1)}, u32[]{:S(2)}, u32[]{:S(2)}) %collective-permute-start.17) | collective-permute-done | bytes 65568 | tf_op jit(solution)/shard_map/ppermute | solution.py:281
  107.9 2.3 %collective-permute-done.16.refs_4_ = bf16[2,128,128]{2,1,0:T(8,128)(2,1)S(1)} collective-permute-done((bf16[2,128,128]{2,1,0:T(8,128)(2,1)S(1)}, bf16[2,128,128]{2,1,0:T(8,128)(2,1)S(1)}, u32[]{:S(2)}, u32[]{:S(2)}) %collective-permute-start.16) | collective-permute-done | bytes 65568 | tf_op jit(solution)/shard_map/ppermute | solution.py:281
  110.2 0.0 copy-done.3
  110.2 0.0 copy-done.4
  110.3 0.6 copy-done.10
  110.9 41.5 %shard_map.86 = (bf16[1,32,128,128]{3,2,1,0:T(8,128)(2,1)}, bf16[1,4,128,128]{3,2,1,0:T(8,128)(2,1)}, bf16[1,4,128,128]{3,2,1,0:T(8,128)(2,1)}) custom-call(s32[3]{0:T(128)} %copy-done.1, bf16[8,128,128]{2,1,0:T(8,128)(2,1)} %copy-done.3, bf16[8,128,128]{2,1,0:T(8,128)(2,1)} %copy-done.4, bf16[8,128,128]{2,1,0:T(8,128)(2,1)} %copy-done.5, ...), custom_call_target="tpu_custom_call" | custom-call | tf_op jit(solution)/shard_map/pallas_call | solution.py:245
  (18 shorter events, 0.2 us)
Async XLA Ops:
  0.6 4.0 %copy-start.2 = (bf16[1,32,128,128]{3,2,1,0:T(8,128)(2,1)S(1)}, bf16[1,32,128,128]{3,2,1,0:T(8,128)(2,1)}, u32[]{:S(2)}) copy-start(bf16[1,32,128,128]{3,2,1,0:T(8,128)(2,1)} %refs_1_.1) | copy-start | bytes 3145732
  2.7 8.3 %collective-permute-start.5 = (bf16[2,128,128]{2,1,0:T(8,128)(2,1)S(1)}, bf16[2,128,128]{2,1,0:T(8,128)(2,1)S(1)}, u32[]{:S(2)}, u32[]{:S(2)}) collective-permute-start(bf16[2,128,128]{2,1,0:T(8,128)(2,1)S(1)} %get-tuple-element.30), channel_id=1, source_target_pairs={{0,6},{2,4},{4,2},{6,0},{8,14},{10,12},{12,10},{14,8},{16,22},{18,... | collective-permute-start | bytes 196616 | tf_op jit(solution)/shard_map/ppermute | solution.py:268
  3.7 7.5 %collective-permute-start.4 = (bf16[2,128,128]{2,1,0:T(8,128)(2,1)S(1)}, bf16[2,128,128]{2,1,0:T(8,128)(2,1)S(1)}, u32[]{:S(2)}, u32[]{:S(2)}) collective-permute-start(bf16[2,128,128]{2,1,0:T(8,128)(2,1)S(1)} %get-tuple-element.31), channel_id=1, source_target_pairs={{0,4},{2,6},{4,0},{6,2},{8,12},{10,14},{12,8},{14,10},{16,20},{18,... | collective-permute-start | bytes 196616 | tf_op jit(solution)/shard_map/ppermute | solution.py:268
  4.3 6.9 %collective-permute-start.3 = (bf16[2,128,128]{2,1,0:T(8,128)(2,1)S(1)}, bf16[2,128,128]{2,1,0:T(8,128)(2,1)S(1)}, u32[]{:S(2)}, u32[]{:S(2)}) collective-permute-start(bf16[2,128,128]{2,1,0:T(8,128)(2,1)S(1)} %get-tuple-element.32), channel_id=1, source_target_pairs={{0,2},{2,0},{4,6},{6,4},{8,10},{10,8},{12,14},{14,12},{16,18},{18,... | collective-permute-start | bytes 196616 | tf_op jit(solution)/shard_map/ppermute | solution.py:268
  4.6 2.0 %copy-start = (bf16[1,32,128,128]{3,2,1,0:T(8,128)(2,1)S(1)}, bf16[1,32,128,128]{3,2,1,0:T(8,128)(2,1)}, u32[]{:S(2)}) copy-start(bf16[1,32,128,128]{3,2,1,0:T(8,128)(2,1)} %refs_0_.1) | copy-start | bytes 3145732
  7.6 33.2 %collective-permute-start = (bf16[17,128,128]{2,1,0:T(8,128)(2,1)}, bf16[17,128,128]{2,1,0:T(8,128)(2,1)S(1)}, u32[]{:S(2)}, u32[]{:S(2)}) collective-permute-start(bf16[17,128,128]{2,1,0:T(8,128)(2,1)} %fusion.3), channel_id=1, source_target_pairs={{0,2},{2,0},{4,6},{6,4},{8,10},{10,8},{12,14},{14,12},{16,18},{18,... | collective-permute-start | bytes 1671176 | tf_op jit(solution)/shard_map/ppermute | solution.py:268
  8.7 32.1 %collective-permute-start.1 = (bf16[17,128,128]{2,1,0:T(8,128)(2,1)}, bf16[17,128,128]{2,1,0:T(8,128)(2,1)S(1)}, u32[]{:S(2)}, u32[]{:S(2)}) collective-permute-start(bf16[17,128,128]{2,1,0:T(8,128)(2,1)} %fusion.4), channel_id=1, source_target_pairs={{0,4},{2,6},{4,0},{6,2},{8,12},{10,14},{12,8},{14,10},{16,20},{18,... | collective-permute-start | bytes 1671176 | tf_op jit(solution)/shard_map/ppermute | solution.py:268
  10.9 29.8 %collective-permute-start.2 = (bf16[17,128,128]{2,1,0:T(8,128)(2,1)}, bf16[17,128,128]{2,1,0:T(8,128)(2,1)S(1)}, u32[]{:S(2)}, u32[]{:S(2)}) collective-permute-start(bf16[17,128,128]{2,1,0:T(8,128)(2,1)} %fusion.5), channel_id=1, source_target_pairs={{0,6},{2,4},{4,2},{6,0},{8,14},{10,12},{12,10},{14,8},{16,22},{18,... | collective-permute-start | bytes 1671176 | tf_op jit(solution)/shard_map/ppermute | solution.py:268
  11.2 2.0 %collective-permute-start.8 = (bf16[2,4,128,128]{3,2,1,0:T(8,128)(2,1)S(1)}, bf16[2,4,128,128]{3,2,1,0:T(8,128)(2,1)S(1)}, u32[]{:S(2)}, u32[]{:S(2)}) collective-permute-start(bf16[2,4,128,128]{3,2,1,0:T(8,128)(2,1)S(1)} %pad_maximum_fusion.refs_6_), channel_id=1, source_target_pairs={{0,24},{2,26},{4,28},{6,30},{1,25},{3,27},{5,29},{7,31}} | collective-permute-start | bytes 786440 | tf_op jit(solution)/shard_map/ppermute | solution.py:273
  11.9 17.9 %collective-permute-start.7 = (bf16[2,4,128,128]{3,2,1,0:T(8,128)(2,1)S(1)}, bf16[2,4,128,128]{3,2,1,0:T(8,128)(2,1)S(1)}, u32[]{:S(2)}, u32[]{:S(2)}) collective-permute-start(bf16[2,4,128,128]{3,2,1,0:T(8,128)(2,1)S(1)} %pad_maximum_fusion.refs_6_), channel_id=1, source_target_pairs={{0,16},{2,18},{4,20},{6,22},{8,24},{10,26},{12,28},{14,30},{1,17},... | collective-permute-start | bytes 786440 | tf_op jit(solution)/shard_map/ppermute | solution.py:273
  13.2 27.5 %collective-permute-start.6 = (bf16[2,4,128,128]{3,2,1,0:T(8,128)(2,1)S(1)}, bf16[2,4,128,128]{3,2,1,0:T(8,128)(2,1)}, u32[]{:S(2)}, u32[]{:S(2)}) collective-permute-start(bf16[2,4,128,128]{3,2,1,0:T(8,128)(2,1)S(1)} %pad_maximum_fusion.refs_6_), channel_id=1, source_target_pairs={{0,8},{2,10},{4,12},{6,14},{8,16},{10,18},{12,20},{14,22},{16,24},... | collective-permute-start | bytes 786440 | tf_op jit(solution)/shard_map/ppermute | solution.py:273
  28.6 40.7 %copy-start.1 = (s32[3]{0:T(128)}, s32[3]{0:T(128)S(1)}, u32[]{:S(2)}) copy-start(s32[3]{0:T(128)S(1)} %pad_add_fusion.meta) | copy-start | bytes 40
  69.3 6.6 %collective-permute-start.15 = (bf16[2,4,128,128]{3,2,0,1:T(8,128)(2,1)S(1)}, bf16[2,4,128,128]{3,2,0,1:T(8,128)(2,1)S(1)}, u32[]{:S(2)}, u32[]{:S(2)}) collective-permute-start(bf16[2,4,128,128]{3,2,0,1:T(8,128)(2,1)S(1)} %copy.12), channel_id=1, source_target_pairs={{24,0},{26,2},{28,4},{30,6},{25,1},{27,3},{29,5},{31,7}} | collective-permute-start | bytes 786440 | tf_op jit(solution)/shard_map/ppermute | solution.py:273
  70.0 15.9 %collective-permute-start.14 = (bf16[2,4,128,128]{3,2,0,1:T(8,128)(2,1)S(1)}, bf16[2,4,128,128]{3,2,0,1:T(8,128)(2,1)S(1)}, u32[]{:S(2)}, u32[]{:S(2)}) collective-permute-start(bf16[2,4,128,128]{3,2,0,1:T(8,128)(2,1)S(1)} %copy.11), channel_id=1, source_target_pairs={{16,0},{18,2},{20,4},{22,6},{24,8},{26,10},{28,12},{30,14},{17,1},... | collective-permute-start | bytes 786440 | tf_op jit(solution)/shard_map/ppermute | solution.py:273
  71.4 20.1 %collective-permute-start.13 = (bf16[2,4,128,128]{3,2,0,1:T(8,128)(2,1)S(1)}, bf16[2,4,128,128]{3,2,0,1:T(8,128)(2,1)S(1)}, u32[]{:S(2)}, u32[]{:S(2)}) collective-permute-start(bf16[2,4,128,128]{3,2,0,1:T(8,128)(2,1)S(1)} %copy.9), channel_id=1, source_target_pairs={{8,0},{10,2},{12,4},{14,6},{16,8},{18,10},{20,12},{22,14},{24,16},... | collective-permute-start | bytes 786440 | tf_op jit(solution)/shard_map/ppermute | solution.py:273
  73.3 19.7 %collective-permute-start.9 = (bf16[8,128,128]{2,1,0:T(8,128)(2,1)S(1)}, bf16[8,128,128]{2,1,0:T(8,128)(2,1)S(1)}, u32[]{:S(2)}, u32[]{:S(2)}) collective-permute-start(bf16[8,128,128]{2,1,0:T(8,128)(2,1)S(1)} %get-tuple-element.11), channel_id=1, source_target_pairs={{1,0},{3,2},{5,4},{7,6},{9,8},{11,10},{13,12},{15,14},{17,16},{19,... | collective-permute-start | bytes 786440 | tf_op jit(solution)/shard_map/ppermute | solution.py:281
  74.6 27.7 %collective-permute-start.10 = (bf16[8,128,128]{2,1,0:T(8,128)(2,1)S(1)}, bf16[8,128,128]{2,1,0:T(8,128)(2,1)S(1)}, u32[]{:S(2)}, u32[]{:S(2)}) collective-permute-start(bf16[8,128,128]{2,1,0:T(8,128)(2,1)S(1)} %get-tuple-element.12), channel_id=1, source_target_pairs={{1,2},{3,0},{5,6},{7,4},{9,10},{11,8},{13,14},{15,12},{17,18},{19,... | collective-permute-start | bytes 786440 | tf_op jit(solution)/shard_map/ppermute | solution.py:281
  75.9 27.7 %collective-permute-start.11 = (bf16[8,128,128]{2,1,0:T(8,128)(2,1)S(1)}, bf16[8,128,128]{2,1,0:T(8,128)(2,1)S(1)}, u32[]{:S(2)}, u32[]{:S(2)}) collective-permute-start(bf16[8,128,128]{2,1,0:T(8,128)(2,1)S(1)} %get-tuple-element.13), channel_id=1, source_target_pairs={{1,4},{3,6},{5,0},{7,2},{9,12},{11,14},{13,8},{15,10},{17,20},{19,... | collective-permute-start | bytes 786440 | tf_op jit(solution)/shard_map/ppermute | solution.py:281
  85.9 19.0 %collective-permute-start.12 = (bf16[8,128,128]{2,1,0:T(8,128)(2,1)S(1)}, bf16[8,128,128]{2,1,0:T(8,128)(2,1)S(1)}, u32[]{:S(2)}, u32[]{:S(2)}) collective-permute-start(bf16[8,128,128]{2,1,0:T(8,128)(2,1)S(1)} %get-tuple-element.14), channel_id=1, source_target_pairs={{1,6},{3,4},{5,2},{7,0},{9,14},{11,12},{13,10},{15,8},{17,22},{19,... | collective-permute-start | bytes 786440 | tf_op jit(solution)/shard_map/ppermute | solution.py:281
  91.7 13.3 %collective-permute-start.19 = (bf16[2,128,128]{2,1,0:T(8,128)(2,1)S(1)}, bf16[2,128,128]{2,1,0:T(8,128)(2,1)S(1)}, u32[]{:S(2)}, u32[]{:S(2)}) collective-permute-start(bf16[2,128,128]{2,1,0:T(8,128)(2,1)S(1)} %get-tuple-element.25), channel_id=1, source_target_pairs={{1,6},{3,4},{5,2},{7,0},{9,14},{11,12},{13,10},{15,8},{17,22},{19,... | collective-permute-start | bytes 196616 | tf_op jit(solution)/shard_map/ppermute | solution.py:281
  93.0 17.2 %copy-start.3 = (bf16[8,128,128]{2,1,0:T(8,128)(2,1)}, bf16[8,128,128]{2,1,0:T(8,128)(2,1)S(1)}, u32[]{:S(2)}) copy-start(bf16[8,128,128]{2,1,0:T(8,128)(2,1)S(1)} %collective-permute-done.9.refs_0_) | copy-start | bytes 786436
  93.0 12.0 %collective-permute-start.18 = (bf16[2,128,128]{2,1,0:T(8,128)(2,1)S(1)}, bf16[2,128,128]{2,1,0:T(8,128)(2,1)S(1)}, u32[]{:S(2)}, u32[]{:S(2)}) collective-permute-start(bf16[2,128,128]{2,1,0:T(8,128)(2,1)S(1)} %get-tuple-element.26), channel_id=1, source_target_pairs={{1,4},{3,6},{5,0},{7,2},{9,12},{11,14},{13,8},{15,10},{17,20},{19,... | collective-permute-start | bytes 196616 | tf_op jit(solution)/shard_map/ppermute | solution.py:281
  102.3 7.9 %copy-start.4 = (bf16[8,128,128]{2,1,0:T(8,128)(2,1)}, bf16[8,128,128]{2,1,0:T(8,128)(2,1)S(1)}, u32[]{:S(2)}) copy-start(bf16[8,128,128]{2,1,0:T(8,128)(2,1)S(1)} %collective-permute-done.10.refs_1_) | copy-start | bytes 786436
  102.3 5.6 %collective-permute-start.17 = (bf16[2,128,128]{2,1,0:T(8,128)(2,1)S(1)}, bf16[2,128,128]{2,1,0:T(8,128)(2,1)S(1)}, u32[]{:S(2)}, u32[]{:S(2)}) collective-permute-start(bf16[2,128,128]{2,1,0:T(8,128)(2,1)S(1)} %get-tuple-element.27), channel_id=1, source_target_pairs={{1,2},{3,0},{5,6},{7,4},{9,10},{11,8},{13,14},{15,12},{17,18},{19,... | collective-permute-start | bytes 196616 | tf_op jit(solution)/shard_map/ppermute | solution.py:281
  103.6 6.6 %copy-start.5 = (bf16[8,128,128]{2,1,0:T(8,128)(2,1)}, bf16[8,128,128]{2,1,0:T(8,128)(2,1)S(1)}, u32[]{:S(2)}) copy-start(bf16[8,128,128]{2,1,0:T(8,128)(2,1)S(1)} %collective-permute-done.11.refs_2_) | copy-start | bytes 786436
  103.7 6.6 %collective-permute-start.16 = (bf16[2,128,128]{2,1,0:T(8,128)(2,1)S(1)}, bf16[2,128,128]{2,1,0:T(8,128)(2,1)S(1)}, u32[]{:S(2)}, u32[]{:S(2)}) collective-permute-start(bf16[2,128,128]{2,1,0:T(8,128)(2,1)S(1)} %get-tuple-element.28), channel_id=1, source_target_pairs={{1,0},{3,2},{5,4},{7,6},{9,8},{11,10},{13,12},{15,14},{17,16},{19,... | collective-permute-start | bytes 196616 | tf_op jit(solution)/shard_map/ppermute | solution.py:281
  105.0 5.3 %copy-start.6 = (bf16[8,128,128]{2,1,0:T(8,128)(2,1)}, bf16[8,128,128]{2,1,0:T(8,128)(2,1)S(1)}, u32[]{:S(2)}) copy-start(bf16[8,128,128]{2,1,0:T(8,128)(2,1)S(1)} %collective-permute-done.12.refs_3_) | copy-start | bytes 786436
  105.0 5.2 %copy-start.7 = (bf16[2,128,128]{2,1,0:T(8,128)(2,1)}, bf16[2,128,128]{2,1,0:T(8,128)(2,1)S(1)}, u32[]{:S(2)}) copy-start(bf16[2,128,128]{2,1,0:T(8,128)(2,1)S(1)} %collective-permute-done.19.refs_7_) | copy-start | bytes 196612
  105.0 5.2 %copy-start.8 = (bf16[2,128,128]{2,1,0:T(8,128)(2,1)}, bf16[2,128,128]{2,1,0:T(8,128)(2,1)S(1)}, u32[]{:S(2)}) copy-start(bf16[2,128,128]{2,1,0:T(8,128)(2,1)S(1)} %collective-permute-done.18.refs_6_) | copy-start | bytes 196612
  107.9 2.3 %copy-start.9 = (bf16[2,128,128]{2,1,0:T(8,128)(2,1)}, bf16[2,128,128]{2,1,0:T(8,128)(2,1)S(1)}, u32[]{:S(2)}) copy-start(bf16[2,128,128]{2,1,0:T(8,128)(2,1)S(1)} %collective-permute-done.17.refs_5_) | copy-start | bytes 196612
  110.3 0.6 copy-start.10

commit v2 on v1

--- a/solution.py
+++ b/solution.py
@@ -245,7 +245,8 @@
     return pl.pallas_call(
         functools.partial(settle_kernel, members, heads),
         out_shape=[jax.ShapeDtypeStruct(shape, jnp.bfloat16) for shape in shapes],
-        in_specs=[pl.BlockSpec(memory_space=pltpu.SMEM)] + [anywhere] * (2 * members),
+        in_specs=[pl.BlockSpec(memory_space=pltpu.SMEM)]
+        + [pl.BlockSpec(memory_space=pltpu.VMEM)] * (2 * members),
         out_specs=[anywhere] * 3,
         scratch_shapes=[pltpu.SemaphoreType.DMA],
     )(meta, *query_parts, *pair_parts)

time: 153 us -> 114 us (0.75)
  Pallas kernels: 70 us -> 30.8 us
    pallas_call x1, Pallas kernels: 41.5 us -> 2.27 us  [settle(): pl.pallas_call(functools.partial(settle_kernel, members, heads), out_shap...]
  transfers between devices with their start and end apart: 20 -> 20, of which waited for: 7 -> 7; matrix products, arithmetic and copies ran while one was open for 4% -> 5% of each run, Pallas kernels for 0% -> 0%
where the time goes in v2:
time: 114 us; the launch traced here: 113 us
  waiting for transfers between devices  38.4 us (34%)
  starting transfers between devices  34.3 us (30%)
  Pallas kernels  30.8 us (27%)
  other arithmetic  5.68 us (5%)
  local copies, waits for them, and re-layouts  2.81 us (2%)
    pallas_call x1, Pallas kernels, attend(): pl.pallas_call(functools.partial(attend_kernel, sizes), out_shape=outs, i...  28.5 us
    ppermute x6, waiting for transfers between devices, along(): return lax.ppermute(tensor, 'seq', route)  25.2 us
    ppermute x6, starting transfers between devices, along(): return lax.ppermute(tensor, 'seq', route)  20.2 us
    ppermute x8, waiting for transfers between devices, previous(): return lax.ppermute(tensor, ('seq', 'pipe'), route)  13.2 us
    ppermute x8, starting transfers between devices, previous(): return lax.ppermute(tensor, ('seq', 'pipe'), route)  10.3 us
    ppermute x6, starting transfers between devices, around(): return lax.ppermute(tensor, 'seq', [(i, i ^ hop) for i in range(devices)])  3.79 us
    concatenate x3, other arithmetic, on_device(): jnp.concatenate([query_part, grad_part, delta_part], axis=0)  2.64 us
  transfers between devices with their start and end apart: 20, of which 7 were waited for; matrix products, arithmetic and copies ran while one was open for 5% of the time, Pallas kernels for 0%

profile of v2, /device:TPU:16, one launch (start us, length us, event | category | flops | bytes accessed | tf_op | source)
XLA Modules:
  0.0 113.2 jit_solution(10694288994461278697)
XLA Ops:
  0.6 0.0 copy-start.2
  0.7 1.0 constant_dynamic-update-slice_fusion.1
  1.7 0.9 constant_dynamic-update-slice_fusion
  2.7 1.0 collective-permute-start.5
  3.7 0.6 collective-permute-start.4
  4.3 0.3 collective-permute-start.3
  4.6 0.0 copy-done.2
  4.6 1.9 %multiply_reduce_fusion = bf16[32,128]{1,0:T(8,128)(2,1)S(1)} fusion(bf16[1,32,128,128]{3,2,1,0:T(8,128)(2,1)} %param.9, bf16[1,32,128,128]{3,2,1,0:T(8,128)(2,1)S(1)} %copy-done.2), kind=kLoop, calls=%fused_computation | loop fusion | flops 2093056 | bytes 2105344 | tf_op jit(solution)/shard_map/reduce_sum | solution.py:298
  6.6 0.0 copy-done
  6.6 0.1 dynamic-slice_bitcast_fusion
  6.7 0.9 fusion.3
  7.6 0.2 collective-permute-start
  7.8 0.9 fusion.4
  8.7 1.4 %collective-permute-start.1 = (bf16[17,128,128]{2,1,0:T(8,128)(2,1)}, bf16[17,128,128]{2,1,0:T(8,128)(2,1)S(1)}, u32[]{:S(2)}, u32[]{:S(2)}) collective-permute-start(bf16[17,128,128]{2,1,0:T(8,128)(2,1)} %fusion.4), channel_id=1, source_target_pairs={{0,4},{2,6},{4,0},{6,2},{8,12},{10,14},{12,8},{14,10},{16,20},{18,... | collective-permute-start | bytes 1671176 | tf_op jit(solution)/shard_map/ppermute | solution.py:269
  10.1 0.9 fusion.5
  10.9 0.0 collective-permute-done.5
  10.9 0.3 collective-permute-start.2
  11.2 0.0 collective-permute-done.4
  11.2 0.0 collective-permute-done.3
  11.2 0.7 collective-permute-start.8
  11.9 1.3 %collective-permute-start.7 = (bf16[2,4,128,128]{3,2,1,0:T(8,128)(2,1)S(1)}, bf16[2,4,128,128]{3,2,1,0:T(8,128)(2,1)S(1)}, u32[]{:S(2)}, u32[]{:S(2)}) collective-permute-start(bf16[2,4,128,128]{3,2,1,0:T(8,128)(2,1)S(1)} %pad_maximum_fusion.refs_6_), channel_id=1, source_target_pairs={{0,16},{2,18},{4,20},{6,22},{8,24},{10,26},{12,28},{14,30},{1,17},... | collective-permute-start | bytes 786440 | tf_op jit(solution)/shard_map/ppermute | solution.py:274
  13.2 0.0 collective-permute-done.8.refs_9_
  13.2 14.4 %collective-permute-start.6 = (bf16[2,4,128,128]{3,2,1,0:T(8,128)(2,1)S(1)}, bf16[2,4,128,128]{3,2,1,0:T(8,128)(2,1)}, u32[]{:S(2)}, u32[]{:S(2)}) collective-permute-start(bf16[2,4,128,128]{3,2,1,0:T(8,128)(2,1)S(1)} %pad_maximum_fusion.refs_6_), channel_id=1, source_target_pairs={{0,8},{2,10},{4,12},{6,14},{8,16},{10,18},{12,20},{14,22},{16,24},... | collective-permute-start | bytes 786440 | tf_op jit(solution)/shard_map/ppermute | solution.py:274
  27.7 0.9 fusion.9
  28.5 0.1 pad_add_fusion.meta
  28.6 1.2 %collective-permute-done.7.refs_8_ = bf16[2,4,128,128]{3,2,1,0:T(8,128)(2,1)S(1)} collective-permute-done((bf16[2,4,128,128]{3,2,1,0:T(8,128)(2,1)S(1)}, bf16[2,4,128,128]{3,2,1,0:T(8,128)(2,1)S(1)}, u32[]{:S(2)}, u32[]{:S(2)}) %collective-permute-start.7) | collective-permute-done | bytes 262176 | tf_op jit(solution)/shard_map/ppermute | solution.py:274
  29.8 10.9 %collective-permute-done.6.refs_7_ = bf16[2,4,128,128]{3,2,1,0:T(8,128)(2,1)} collective-permute-done((bf16[2,4,128,128]{3,2,1,0:T(8,128)(2,1)S(1)}, bf16[2,4,128,128]{3,2,1,0:T(8,128)(2,1)}, u32[]{:S(2)}, u32[]{:S(2)}) %collective-permute-start.6) | collective-permute-done | bytes 262176 | tf_op jit(solution)/shard_map/ppermute | solution.py:274
  40.8 0.0 collective-permute-done.refs_3_
  40.8 0.0 collective-permute-done.1.refs_4_
  40.8 0.0 collective-permute-done.2.refs_5_
  40.8 28.5 %shard_map.85 = (bf16[8,128,128]{2,1,0:T(8,128)(2,1)S(1)}, bf16[8,128,128]{2,1,0:T(8,128)(2,1)S(1)}, bf16[8,128,128]{2,1,0:T(8,128)(2,1)S(1)}, bf16[8,128,128]{2...) custom-call(s32[3]{0:T(128)S(1)} %pad_add_fusion.meta, ...), custom_call_target="tpu_custom_call" | custom-call | tf_op jit(solution)/shard_map/pallas_call | solution.py:191
  69.3 0.0 copy-done.1
  69.3 0.7 collective-permute-start.15
  70.0 1.3 %collective-permute-start.14 = (bf16[2,4,128,128]{3,2,0,1:T(8,128)(2,1)S(1)}, bf16[2,4,128,128]{3,2,0,1:T(8,128)(2,1)S(1)}, u32[]{:S(2)}, u32[]{:S(2)}) collective-permute-start(bf16[2,4,128,128]{3,2,0,1:T(8,128)(2,1)S(1)} %copy.11), channel_id=1, source_target_pairs={{16,0},{18,2},{20,4},{22,6},{24,8},{26,10},{28,12},{30,14},{17,1},... | collective-permute-start | bytes 786440 | tf_op jit(solution)/shard_map/ppermute | solution.py:274
  71.4 1.9 %collective-permute-start.13 = (bf16[2,4,128,128]{3,2,0,1:T(8,128)(2,1)S(1)}, bf16[2,4,128,128]{3,2,0,1:T(8,128)(2,1)S(1)}, u32[]{:S(2)}, u32[]{:S(2)}) collective-permute-start(bf16[2,4,128,128]{3,2,0,1:T(8,128)(2,1)S(1)} %copy.9), channel_id=1, source_target_pairs={{8,0},{10,2},{12,4},{14,6},{16,8},{18,10},{20,12},{22,14},{24,16},... | collective-permute-start | bytes 786440 | tf_op jit(solution)/shard_map/ppermute | solution.py:274
  73.3 1.3 %collective-permute-start.9 = (bf16[8,128,128]{2,1,0:T(8,128)(2,1)S(1)}, bf16[8,128,128]{2,1,0:T(8,128)(2,1)S(1)}, u32[]{:S(2)}, u32[]{:S(2)}) collective-permute-start(bf16[8,128,128]{2,1,0:T(8,128)(2,1)S(1)} %get-tuple-element.11), channel_id=1, source_target_pairs={{1,0},{3,2},{5,4},{7,6},{9,8},{11,10},{13,12},{15,14},{17,16},{19,... | collective-permute-start | bytes 786440 | tf_op jit(solution)/shard_map/ppermute | solution.py:282
  74.6 1.3 %collective-permute-start.10 = (bf16[8,128,128]{2,1,0:T(8,128)(2,1)S(1)}, bf16[8,128,128]{2,1,0:T(8,128)(2,1)S(1)}, u32[]{:S(2)}, u32[]{:S(2)}) collective-permute-start(bf16[8,128,128]{2,1,0:T(8,128)(2,1)S(1)} %get-tuple-element.12), channel_id=1, source_target_pairs={{1,2},{3,0},{5,6},{7,4},{9,10},{11,8},{13,14},{15,12},{17,18},{19,... | collective-permute-start | bytes 786440 | tf_op jit(solution)/shard_map/ppermute | solution.py:282
  75.9 0.0 collective-permute-done.15
  75.9 1.3 %collective-permute-start.11 = (bf16[8,128,128]{2,1,0:T(8,128)(2,1)S(1)}, bf16[8,128,128]{2,1,0:T(8,128)(2,1)S(1)}, u32[]{:S(2)}, u32[]{:S(2)}) collective-permute-start(bf16[8,128,128]{2,1,0:T(8,128)(2,1)S(1)} %get-tuple-element.13), channel_id=1, source_target_pairs={{1,4},{3,6},{5,0},{7,2},{9,12},{11,14},{13,8},{15,10},{17,20},{19,... | collective-permute-start | bytes 786440 | tf_op jit(solution)/shard_map/ppermute | solution.py:282
  77.2 8.7 %collective-permute-done.14 = bf16[2,4,128,128]{3,2,0,1:T(8,128)(2,1)S(1)} collective-permute-done((bf16[2,4,128,128]{3,2,0,1:T(8,128)(2,1)S(1)}, bf16[2,4,128,128]{3,2,0,1:T(8,128)(2,1)S(1)}, u32[]{:S(2)}, u32[]{:S(2)}) %collective-permute-start.14) | collective-permute-done | bytes 262176 | tf_op jit(solution)/shard_map/ppermute | solution.py:274
  85.9 1.3 %collective-permute-start.12 = (bf16[8,128,128]{2,1,0:T(8,128)(2,1)S(1)}, bf16[8,128,128]{2,1,0:T(8,128)(2,1)S(1)}, u32[]{:S(2)}, u32[]{:S(2)}) collective-permute-start(bf16[8,128,128]{2,1,0:T(8,128)(2,1)S(1)} %get-tuple-element.14), channel_id=1, source_target_pairs={{1,6},{3,4},{5,2},{7,0},{9,14},{11,12},{13,10},{15,8},{17,22},{19,... | collective-permute-start | bytes 786440 | tf_op jit(solution)/shard_map/ppermute | solution.py:282
  87.2 4.3 %collective-permute-done.13 = bf16[2,4,128,128]{3,2,0,1:T(8,128)(2,1)S(1)} collective-permute-done((bf16[2,4,128,128]{3,2,0,1:T(8,128)(2,1)S(1)}, bf16[2,4,128,128]{3,2,0,1:T(8,128)(2,1)S(1)}, u32[]{:S(2)}, u32[]{:S(2)}) %collective-permute-start.13) | collective-permute-done | bytes 262176 | tf_op jit(solution)/shard_map/ppermute | solution.py:274
  91.5 0.1 fusion.8
  91.7 1.3 %collective-permute-start.19 = (bf16[2,128,128]{2,1,0:T(8,128)(2,1)S(1)}, bf16[2,128,128]{2,1,0:T(8,128)(2,1)S(1)}, u32[]{:S(2)}, u32[]{:S(2)}) collective-permute-start(bf16[2,128,128]{2,1,0:T(8,128)(2,1)S(1)} %get-tuple-element.25), channel_id=1, source_target_pairs={{1,6},{3,4},{5,2},{7,0},{9,14},{11,12},{13,10},{15,8},{17,22},{19,... | collective-permute-start | bytes 196616 | tf_op jit(solution)/shard_map/ppermute | solution.py:282
  93.0 0.0 collective-permute-done.9.refs_0_
  93.0 0.0 copy-start.3
  93.0 1.3 %collective-permute-start.18 = (bf16[2,128,128]{2,1,0:T(8,128)(2,1)S(1)}, bf16[2,128,128]{2,1,0:T(8,128)(2,1)S(1)}, u32[]{:S(2)}, u32[]{:S(2)}) collective-permute-start(bf16[2,128,128]{2,1,0:T(8,128)(2,1)S(1)} %get-tuple-element.26), channel_id=1, source_target_pairs={{1,4},{3,6},{5,0},{7,2},{9,12},{11,14},{13,8},{15,10},{17,20},{19,... | collective-permute-start | bytes 196616 | tf_op jit(solution)/shard_map/ppermute | solution.py:282
  94.3 8.0 %collective-permute-done.10.refs_1_ = bf16[8,128,128]{2,1,0:T(8,128)(2,1)S(1)} collective-permute-done((bf16[8,128,128]{2,1,0:T(8,128)(2,1)S(1)}, bf16[8,128,128]{2,1,0:T(8,128)(2,1)S(1)}, u32[]{:S(2)}, u32[]{:S(2)}) %collective-permute-start.10) | collective-permute-done | bytes 262176 | tf_op jit(solution)/shard_map/ppermute | solution.py:282
  102.3 1.3 %collective-permute-start.17 = (bf16[2,128,128]{2,1,0:T(8,128)(2,1)S(1)}, bf16[2,128,128]{2,1,0:T(8,128)(2,1)S(1)}, u32[]{:S(2)}, u32[]{:S(2)}) collective-permute-start(bf16[2,128,128]{2,1,0:T(8,128)(2,1)S(1)} %get-tuple-element.27), channel_id=1, source_target_pairs={{1,2},{3,0},{5,6},{7,4},{9,10},{11,8},{13,14},{15,12},{17,18},{19,... | collective-permute-start | bytes 196616 | tf_op jit(solution)/shard_map/ppermute | solution.py:282
  103.6 0.0 collective-permute-done.11.refs_2_
  103.6 0.0 copy-start.5
  103.7 1.3 %collective-permute-start.16 = (bf16[2,128,128]{2,1,0:T(8,128)(2,1)S(1)}, bf16[2,128,128]{2,1,0:T(8,128)(2,1)S(1)}, u32[]{:S(2)}, u32[]{:S(2)}) collective-permute-start(bf16[2,128,128]{2,1,0:T(8,128)(2,1)S(1)} %get-tuple-element.28), channel_id=1, source_target_pairs={{1,0},{3,2},{5,4},{7,6},{9,8},{11,10},{13,12},{15,14},{17,16},{19,... | collective-permute-start | bytes 196616 | tf_op jit(solution)/shard_map/ppermute | solution.py:282
  105.0 0.0 collective-permute-done.12.refs_3_
  105.0 0.0 copy-start.6
  105.0 0.0 collective-permute-done.19.refs_7_
  105.0 0.0 copy-start.7
  105.0 0.0 collective-permute-done.18.refs_6_
  105.0 0.0 copy-start.8
  105.0 2.9 %collective-permute-done.17.refs_5_ = bf16[2,128,128]{2,1,0:T(8,128)(2,1)S(1)} collective-permute-done((bf16[2,128,128]{2,1,0:T(8,128)(2,1)S(1)}, bf16[2,128,128]{2,1,0:T(8,128)(2,1)S(1)}, u32[]{:S(2)}, u32[]{:S(2)}) %collective-permute-start.17) | collective-permute-done | bytes 65568 | tf_op jit(solution)/shard_map/ppermute | solution.py:282
  107.9 2.3 %collective-permute-done.16.refs_4_ = bf16[2,128,128]{2,1,0:T(8,128)(2,1)S(1)} collective-permute-done((bf16[2,128,128]{2,1,0:T(8,128)(2,1)S(1)}, bf16[2,128,128]{2,1,0:T(8,128)(2,1)S(1)}, u32[]{:S(2)}, u32[]{:S(2)}) %collective-permute-start.16) | collective-permute-done | bytes 65568 | tf_op jit(solution)/shard_map/ppermute | solution.py:282
  110.2 0.0 copy-done.3
  110.2 0.0 copy-done.4
  110.3 0.6 copy-done.10
  110.9 2.3 %shard_map.86 = (bf16[1,32,128,128]{3,2,1,0:T(8,128)(2,1)}, bf16[1,4,128,128]{3,2,1,0:T(8,128)(2,1)}, bf16[1,4,128,128]{3,2,1,0:T(8,128)(2,1)}) custom-call(s32[3]{0:T(128)} %copy-done.1, bf16[8,128,128]{2,1,0:T(8,128)(2,1)} %copy-done.3, bf16[8,128,128]{2,1,0:T(8,128)(2,1)} %copy-done.4, bf16[8,128,128]{2,1,0:T(8,128)(2,1)} %copy-done.5, ...), custom_call_target="tpu_custom_call" | custom-call | tf_op jit(solution)/shard_map/pallas_call | solution.py:245
  (18 shorter events, 0.2 us)
Async XLA Ops:
  0.6 4.0 %copy-start.2 = (bf16[1,32,128,128]{3,2,1,0:T(8,128)(2,1)S(1)}, bf16[1,32,128,128]{3,2,1,0:T(8,128)(2,1)}, u32[]{:S(2)}) copy-start(bf16[1,32,128,128]{3,2,1,0:T(8,128)(2,1)} %refs_1_.1) | copy-start | bytes 3145732
  2.7 8.3 %collective-permute-start.5 = (bf16[2,128,128]{2,1,0:T(8,128)(2,1)S(1)}, bf16[2,128,128]{2,1,0:T(8,128)(2,1)S(1)}, u32[]{:S(2)}, u32[]{:S(2)}) collective-permute-start(bf16[2,128,128]{2,1,0:T(8,128)(2,1)S(1)} %get-tuple-element.30), channel_id=1, source_target_pairs={{0,6},{2,4},{4,2},{6,0},{8,14},{10,12},{12,10},{14,8},{16,22},{18,... | collective-permute-start | bytes 196616 | tf_op jit(solution)/shard_map/ppermute | solution.py:269
  3.7 7.5 %collective-permute-start.4 = (bf16[2,128,128]{2,1,0:T(8,128)(2,1)S(1)}, bf16[2,128,128]{2,1,0:T(8,128)(2,1)S(1)}, u32[]{:S(2)}, u32[]{:S(2)}) collective-permute-start(bf16[2,128,128]{2,1,0:T(8,128)(2,1)S(1)} %get-tuple-element.31), channel_id=1, source_target_pairs={{0,4},{2,6},{4,0},{6,2},{8,12},{10,14},{12,8},{14,10},{16,20},{18,... | collective-permute-start | bytes 196616 | tf_op jit(solution)/shard_map/ppermute | solution.py:269
  4.3 6.9 %collective-permute-start.3 = (bf16[2,128,128]{2,1,0:T(8,128)(2,1)S(1)}, bf16[2,128,128]{2,1,0:T(8,128)(2,1)S(1)}, u32[]{:S(2)}, u32[]{:S(2)}) collective-permute-start(bf16[2,128,128]{2,1,0:T(8,128)(2,1)S(1)} %get-tuple-element.32), channel_id=1, source_target_pairs={{0,2},{2,0},{4,6},{6,4},{8,10},{10,8},{12,14},{14,12},{16,18},{18,... | collective-permute-start | bytes 196616 | tf_op jit(solution)/shard_map/ppermute | solution.py:269
  4.6 2.0 %copy-start = (bf16[1,32,128,128]{3,2,1,0:T(8,128)(2,1)S(1)}, bf16[1,32,128,128]{3,2,1,0:T(8,128)(2,1)}, u32[]{:S(2)}) copy-start(bf16[1,32,128,128]{3,2,1,0:T(8,128)(2,1)} %refs_0_.1) | copy-start | bytes 3145732
  7.6 33.2 %collective-permute-start = (bf16[17,128,128]{2,1,0:T(8,128)(2,1)}, bf16[17,128,128]{2,1,0:T(8,128)(2,1)S(1)}, u32[]{:S(2)}, u32[]{:S(2)}) collective-permute-start(bf16[17,128,128]{2,1,0:T(8,128)(2,1)} %fusion.3), channel_id=1, source_target_pairs={{0,2},{2,0},{4,6},{6,4},{8,10},{10,8},{12,14},{14,12},{16,18},{18,... | collective-permute-start | bytes 1671176 | tf_op jit(solution)/shard_map/ppermute | solution.py:269
  8.7 32.1 %collective-permute-start.1 = (bf16[17,128,128]{2,1,0:T(8,128)(2,1)}, bf16[17,128,128]{2,1,0:T(8,128)(2,1)S(1)}, u32[]{:S(2)}, u32[]{:S(2)}) collective-permute-start(bf16[17,128,128]{2,1,0:T(8,128)(2,1)} %fusion.4), channel_id=1, source_target_pairs={{0,4},{2,6},{4,0},{6,2},{8,12},{10,14},{12,8},{14,10},{16,20},{18,... | collective-permute-start | bytes 1671176 | tf_op jit(solution)/shard_map/ppermute | solution.py:269
  10.9 29.8 %collective-permute-start.2 = (bf16[17,128,128]{2,1,0:T(8,128)(2,1)}, bf16[17,128,128]{2,1,0:T(8,128)(2,1)S(1)}, u32[]{:S(2)}, u32[]{:S(2)}) collective-permute-start(bf16[17,128,128]{2,1,0:T(8,128)(2,1)} %fusion.5), channel_id=1, source_target_pairs={{0,6},{2,4},{4,2},{6,0},{8,14},{10,12},{12,10},{14,8},{16,22},{18,... | collective-permute-start | bytes 1671176 | tf_op jit(solution)/shard_map/ppermute | solution.py:269
  11.2 2.0 %collective-permute-start.8 = (bf16[2,4,128,128]{3,2,1,0:T(8,128)(2,1)S(1)}, bf16[2,4,128,128]{3,2,1,0:T(8,128)(2,1)S(1)}, u32[]{:S(2)}, u32[]{:S(2)}) collective-permute-start(bf16[2,4,128,128]{3,2,1,0:T(8,128)(2,1)S(1)} %pad_maximum_fusion.refs_6_), channel_id=1, source_target_pairs={{0,24},{2,26},{4,28},{6,30},{1,25},{3,27},{5,29},{7,31}} | collective-permute-start | bytes 786440 | tf_op jit(solution)/shard_map/ppermute | solution.py:274
  11.9 17.9 %collective-permute-start.7 = (bf16[2,4,128,128]{3,2,1,0:T(8,128)(2,1)S(1)}, bf16[2,4,128,128]{3,2,1,0:T(8,128)(2,1)S(1)}, u32[]{:S(2)}, u32[]{:S(2)}) collective-permute-start(bf16[2,4,128,128]{3,2,1,0:T(8,128)(2,1)S(1)} %pad_maximum_fusion.refs_6_), channel_id=1, source_target_pairs={{0,16},{2,18},{4,20},{6,22},{8,24},{10,26},{12,28},{14,30},{1,17},... | collective-permute-start | bytes 786440 | tf_op jit(solution)/shard_map/ppermute | solution.py:274
  13.2 27.5 %collective-permute-start.6 = (bf16[2,4,128,128]{3,2,1,0:T(8,128)(2,1)S(1)}, bf16[2,4,128,128]{3,2,1,0:T(8,128)(2,1)}, u32[]{:S(2)}, u32[]{:S(2)}) collective-permute-start(bf16[2,4,128,128]{3,2,1,0:T(8,128)(2,1)S(1)} %pad_maximum_fusion.refs_6_), channel_id=1, source_target_pairs={{0,8},{2,10},{4,12},{6,14},{8,16},{10,18},{12,20},{14,22},{16,24},... | collective-permute-start | bytes 786440 | tf_op jit(solution)/shard_map/ppermute | solution.py:274
  28.6 40.7 %copy-start.1 = (s32[3]{0:T(128)}, s32[3]{0:T(128)S(1)}, u32[]{:S(2)}) copy-start(s32[3]{0:T(128)S(1)} %pad_add_fusion.meta) | copy-start | bytes 40
  69.3 6.6 %collective-permute-start.15 = (bf16[2,4,128,128]{3,2,0,1:T(8,128)(2,1)S(1)}, bf16[2,4,128,128]{3,2,0,1:T(8,128)(2,1)S(1)}, u32[]{:S(2)}, u32[]{:S(2)}) collective-permute-start(bf16[2,4,128,128]{3,2,0,1:T(8,128)(2,1)S(1)} %copy.12), channel_id=1, source_target_pairs={{24,0},{26,2},{28,4},{30,6},{25,1},{27,3},{29,5},{31,7}} | collective-permute-start | bytes 786440 | tf_op jit(solution)/shard_map/ppermute | solution.py:274
  70.0 15.9 %collective-permute-start.14 = (bf16[2,4,128,128]{3,2,0,1:T(8,128)(2,1)S(1)}, bf16[2,4,128,128]{3,2,0,1:T(8,128)(2,1)S(1)}, u32[]{:S(2)}, u32[]{:S(2)}) collective-permute-start(bf16[2,4,128,128]{3,2,0,1:T(8,128)(2,1)S(1)} %copy.11), channel_id=1, source_target_pairs={{16,0},{18,2},{20,4},{22,6},{24,8},{26,10},{28,12},{30,14},{17,1},... | collective-permute-start | bytes 786440 | tf_op jit(solution)/shard_map/ppermute | solution.py:274
  71.4 20.1 %collective-permute-start.13 = (bf16[2,4,128,128]{3,2,0,1:T(8,128)(2,1)S(1)}, bf16[2,4,128,128]{3,2,0,1:T(8,128)(2,1)S(1)}, u32[]{:S(2)}, u32[]{:S(2)}) collective-permute-start(bf16[2,4,128,128]{3,2,0,1:T(8,128)(2,1)S(1)} %copy.9), channel_id=1, source_target_pairs={{8,0},{10,2},{12,4},{14,6},{16,8},{18,10},{20,12},{22,14},{24,16},... | collective-permute-start | bytes 786440 | tf_op jit(solution)/shard_map/ppermute | solution.py:274
  73.3 19.7 %collective-permute-start.9 = (bf16[8,128,128]{2,1,0:T(8,128)(2,1)S(1)}, bf16[8,128,128]{2,1,0:T(8,128)(2,1)S(1)}, u32[]{:S(2)}, u32[]{:S(2)}) collective-permute-start(bf16[8,128,128]{2,1,0:T(8,128)(2,1)S(1)} %get-tuple-element.11), channel_id=1, source_target_pairs={{1,0},{3,2},{5,4},{7,6},{9,8},{11,10},{13,12},{15,14},{17,16},{19,... | collective-permute-start | bytes 786440 | tf_op jit(solution)/shard_map/ppermute | solution.py:282
  74.6 27.7 %collective-permute-start.10 = (bf16[8,128,128]{2,1,0:T(8,128)(2,1)S(1)}, bf16[8,128,128]{2,1,0:T(8,128)(2,1)S(1)}, u32[]{:S(2)}, u32[]{:S(2)}) collective-permute-start(bf16[8,128,128]{2,1,0:T(8,128)(2,1)S(1)} %get-tuple-element.12), channel_id=1, source_target_pairs={{1,2},{3,0},{5,6},{7,4},{9,10},{11,8},{13,14},{15,12},{17,18},{19,... | collective-permute-start | bytes 786440 | tf_op jit(solution)/shard_map/ppermute | solution.py:282
  75.9 27.7 %collective-permute-start.11 = (bf16[8,128,128]{2,1,0:T(8,128)(2,1)S(1)}, bf16[8,128,128]{2,1,0:T(8,128)(2,1)S(1)}, u32[]{:S(2)}, u32[]{:S(2)}) collective-permute-start(bf16[8,128,128]{2,1,0:T(8,128)(2,1)S(1)} %get-tuple-element.13), channel_id=1, source_target_pairs={{1,4},{3,6},{5,0},{7,2},{9,12},{11,14},{13,8},{15,10},{17,20},{19,... | collective-permute-start | bytes 786440 | tf_op jit(solution)/shard_map/ppermute | solution.py:282
  85.9 19.0 %collective-permute-start.12 = (bf16[8,128,128]{2,1,0:T(8,128)(2,1)S(1)}, bf16[8,128,128]{2,1,0:T(8,128)(2,1)S(1)}, u32[]{:S(2)}, u32[]{:S(2)}) collective-permute-start(bf16[8,128,128]{2,1,0:T(8,128)(2,1)S(1)} %get-tuple-element.14), channel_id=1, source_target_pairs={{1,6},{3,4},{5,2},{7,0},{9,14},{11,12},{13,10},{15,8},{17,22},{19,... | collective-permute-start | bytes 786440 | tf_op jit(solution)/shard_map/ppermute | solution.py:282
  91.7 13.3 %collective-permute-start.19 = (bf16[2,128,128]{2,1,0:T(8,128)(2,1)S(1)}, bf16[2,128,128]{2,1,0:T(8,128)(2,1)S(1)}, u32[]{:S(2)}, u32[]{:S(2)}) collective-permute-start(bf16[2,128,128]{2,1,0:T(8,128)(2,1)S(1)} %get-tuple-element.25), channel_id=1, source_target_pairs={{1,6},{3,4},{5,2},{7,0},{9,14},{11,12},{13,10},{15,8},{17,22},{19,... | collective-permute-start | bytes 196616 | tf_op jit(solution)/shard_map/ppermute | solution.py:282
  93.0 17.2 %copy-start.3 = (bf16[8,128,128]{2,1,0:T(8,128)(2,1)}, bf16[8,128,128]{2,1,0:T(8,128)(2,1)S(1)}, u32[]{:S(2)}) copy-start(bf16[8,128,128]{2,1,0:T(8,128)(2,1)S(1)} %collective-permute-done.9.refs_0_) | copy-start | bytes 786436
  93.0 12.0 %collective-permute-start.18 = (bf16[2,128,128]{2,1,0:T(8,128)(2,1)S(1)}, bf16[2,128,128]{2,1,0:T(8,128)(2,1)S(1)}, u32[]{:S(2)}, u32[]{:S(2)}) collective-permute-start(bf16[2,128,128]{2,1,0:T(8,128)(2,1)S(1)} %get-tuple-element.26), channel_id=1, source_target_pairs={{1,4},{3,6},{5,0},{7,2},{9,12},{11,14},{13,8},{15,10},{17,20},{19,... | collective-permute-start | bytes 196616 | tf_op jit(solution)/shard_map/ppermute | solution.py:282
  102.3 7.9 %copy-start.4 = (bf16[8,128,128]{2,1,0:T(8,128)(2,1)}, bf16[8,128,128]{2,1,0:T(8,128)(2,1)S(1)}, u32[]{:S(2)}) copy-start(bf16[8,128,128]{2,1,0:T(8,128)(2,1)S(1)} %collective-permute-done.10.refs_1_) | copy-start | bytes 786436
  102.3 5.6 %collective-permute-start.17 = (bf16[2,128,128]{2,1,0:T(8,128)(2,1)S(1)}, bf16[2,128,128]{2,1,0:T(8,128)(2,1)S(1)}, u32[]{:S(2)}, u32[]{:S(2)}) collective-permute-start(bf16[2,128,128]{2,1,0:T(8,128)(2,1)S(1)} %get-tuple-element.27), channel_id=1, source_target_pairs={{1,2},{3,0},{5,6},{7,4},{9,10},{11,8},{13,14},{15,12},{17,18},{19,... | collective-permute-start | bytes 196616 | tf_op jit(solution)/shard_map/ppermute | solution.py:282
  103.6 6.6 %copy-start.5 = (bf16[8,128,128]{2,1,0:T(8,128)(2,1)}, bf16[8,128,128]{2,1,0:T(8,128)(2,1)S(1)}, u32[]{:S(2)}) copy-start(bf16[8,128,128]{2,1,0:T(8,128)(2,1)S(1)} %collective-permute-done.11.refs_2_) | copy-start | bytes 786436
  103.7 6.6 %collective-permute-start.16 = (bf16[2,128,128]{2,1,0:T(8,128)(2,1)S(1)}, bf16[2,128,128]{2,1,0:T(8,128)(2,1)S(1)}, u32[]{:S(2)}, u32[]{:S(2)}) collective-permute-start(bf16[2,128,128]{2,1,0:T(8,128)(2,1)S(1)} %get-tuple-element.28), channel_id=1, source_target_pairs={{1,0},{3,2},{5,4},{7,6},{9,8},{11,10},{13,12},{15,14},{17,16},{19,... | collective-permute-start | bytes 196616 | tf_op jit(solution)/shard_map/ppermute | solution.py:282
  105.0 5.3 %copy-start.6 = (bf16[8,128,128]{2,1,0:T(8,128)(2,1)}, bf16[8,128,128]{2,1,0:T(8,128)(2,1)S(1)}, u32[]{:S(2)}) copy-start(bf16[8,128,128]{2,1,0:T(8,128)(2,1)S(1)} %collective-permute-done.12.refs_3_) | copy-start | bytes 786436
  105.0 5.2 %copy-start.7 = (bf16[2,128,128]{2,1,0:T(8,128)(2,1)}, bf16[2,128,128]{2,1,0:T(8,128)(2,1)S(1)}, u32[]{:S(2)}) copy-start(bf16[2,128,128]{2,1,0:T(8,128)(2,1)S(1)} %collective-permute-done.19.refs_7_) | copy-start | bytes 196612
  105.0 5.2 %copy-start.8 = (bf16[2,128,128]{2,1,0:T(8,128)(2,1)}, bf16[2,128,128]{2,1,0:T(8,128)(2,1)S(1)}, u32[]{:S(2)}) copy-start(bf16[2,128,128]{2,1,0:T(8,128)(2,1)S(1)} %collective-permute-done.18.refs_6_) | copy-start | bytes 196612
  107.9 2.3 %copy-start.9 = (bf16[2,128,128]{2,1,0:T(8,128)(2,1)}, bf16[2,128,128]{2,1,0:T(8,128)(2,1)S(1)}, u32[]{:S(2)}) copy-start(bf16[2,128,128]{2,1,0:T(8,128)(2,1)S(1)} %collective-permute-done.17.refs_5_) | copy-start | bytes 196612
  110.3 0.6 copy-start.10

commit v3 on v2

v3 whole, which is shorter than its diff:
```python
import functools
import math

import jax
import jax.numpy as jnp
from jax import lax
from jax.experimental import pallas as pl
from jax.experimental.pallas import tpu as pltpu
from jax.sharding import PartitionSpec as P

BLK = 512
TILE_HEADS = 2
FAR = 1e30


def nt(a, b):
    return lax.dot_general(a, b, (((1,), (1,)), ((), ())), preferred_element_type=jnp.float32)


def nn(a, b):
    return lax.dot_general(a, b, (((1,), (0,)), ((), ())), preferred_element_type=jnp.float32)


def tn(a, b):
    return lax.dot_general(a, b, (((0,), (0,)), ((), ())), preferred_element_type=jnp.float32)


def attend_kernel(sizes, meta, queries, grads, deltas, pack, pairs, twins, *refs):
    heads, rows, feature = sizes
    (query_outs, pair_keep, pair_give, query_buf, grad_buf, low_buf, delta_buf, pair_buf,
     key_acc, value_acc, query_done, keep_done, give_done, in_sem, out_sem) = (refs[:2],) + refs[2:]
    side, core, head = meta[0], meta[1], meta[2]
    offsets = (meta[3], meta[4])
    lanes = TILE_HEADS * rows
    factor = feature ** (-0.5)
    sharp = factor * math.log2(math.e)

    loads = []
    for hop in range(2):
        spot = 2 * (side ^ hop)
        loads.append((pairs.at[0, :, hop], pair_buf.at[2, :, spot + core]))
        loads.append((twins.at[0, :, hop], pair_buf.at[2, :, spot + 1 - core]))
    for slot in range(2):
        loads.append((pairs.at[offsets[slot]], pair_buf.at[slot, :, pl.ds(0, 2)]))
        loads.append((twins.at[offsets[slot]], pair_buf.at[slot, :, pl.ds(2, 2)]))
    first = pl.ds(head * heads, heads)
    loads.append((queries.at[0, first], query_buf.at[side]))
    loads.append((grads.at[0, first], grad_buf.at[side]))
    loads.append((deltas.at[head], low_buf.at[side]))
    loads.append((pack.at[pl.ds(0, heads)], query_buf.at[1 - side]))
    loads.append((pack.at[pl.ds(heads, heads)], grad_buf.at[1 - side]))
    loads.append((pack.at[2 * heads, pl.ds(0, 16)], low_buf.at[1 - side]))
    copies = [
        pltpu.make_async_copy(source, target, in_sem.at[i])
        for i, (source, target) in enumerate(loads)
    ]
    for copy in copies:
        copy.start()
    key_acc[...] = jnp.zeros_like(key_acc)
    value_acc[...] = jnp.zeros_like(value_acc)
    for copy in copies:
        copy.wait()
    delta_buf[...] = low_buf[...].astype(jnp.float32)

    biases = [jnp.where(offset > 0, 0.0, FAR) for offset in offsets]
    edge_rows = 2 * rows
    key_ids = lax.broadcasted_iota(jnp.int32, (edge_rows, lanes), 0)
    row_ids = lax.broadcasted_iota(jnp.int32, (edge_rows, lanes), 1) % rows
    causal = key_ids <= row_ids + core * rows

    for half in range(2):
        visible = (half + 1) * edge_rows
        spans = [(0, BLK), (1, BLK), (2, visible)]

        def tile(step, carry, half=half, visible=visible, spans=spans):
            here = pl.ds(step * TILE_HEADS, TILE_HEADS)
            query = query_buf[half, here].reshape(lanes, feature)
            grad = grad_buf[half, here].reshape(lanes, feature)
            delta = jnp.concatenate(
                [
                    delta_buf[half, pl.ds(step * TILE_HEADS + i, 1), :]
                    for i in range(TILE_HEADS)
                ],
                axis=1,
            )

            def fetch(part, slot, length):
                return pair_buf[slot, part].reshape(BLK, feature)[:length]

            scores = [nt(fetch(0, slot, length), query) for slot, length in spans]
            edge = jnp.where(causal, scores[2][visible - edge_rows :], -FAR)
            scores[2] = (
                edge
                if half == 0
                else jnp.concatenate([scores[2][: visible - edge_rows], edge], axis=0)
            )
            tops = [jnp.max(score, axis=0, keepdims=True) for score in scores]
            top = jnp.maximum(jnp.maximum(tops[0] - biases[0], tops[1] - biases[1]), tops[2])
            shifts = [top + biases[0], top + biases[1], top]
            raws = [jnp.exp2((score - shift) * sharp) for score, shift in zip(scores, shifts)]
            total = sum(jnp.sum(raw, axis=0, keepdims=True) for raw in raws)
            inverse = 1.0 / total
            query_sum = jnp.zeros((lanes, feature), jnp.float32)
            for (slot, length), raw in zip(spans, raws):
                dprobs = nt(fetch(1, slot, length), grad)
                probs = raw * inverse
                dscores = (probs * (dprobs - delta)).astype(jnp.bfloat16)
                base = slot * BLK
                value_acc[base : base + length] += nn(probs.astype(jnp.bfloat16), grad)
                key_acc[base : base + length] += nn(dscores, query)
                query_sum += tn(dscores, fetch(0, slot, length))
            query_done[half, here] = (
                (query_sum * factor).astype(jnp.bfloat16).reshape(TILE_HEADS, rows, feature)
            )
            return carry

        lax.fori_loop(0, heads // TILE_HEADS, tile, 0)

    stores = [
        (query_done.at[side], query_outs[0]),
        (query_done.at[1 - side], query_outs[1]),
    ]
    shape = (2, rows, feature)
    for part, acc, scale in ((0, key_acc, factor), (1, value_acc, 1.0)):
        for slot in range(2):
            keep = slice(slot * BLK, slot * BLK + 2 * rows)
            give = slice(slot * BLK + 2 * rows, (slot + 1) * BLK)
            keep_done[slot, part] = (acc[keep] * scale).reshape(shape)
            give_done[slot, part] = (acc[give] * scale).astype(jnp.bfloat16).reshape(shape)
        for hop in range(2):
            spot = 2 * (side ^ hop)
            start = pl.multiple_of(2 * BLK + (spot + core) * rows, rows)
            keep_done[2, part, hop] = acc[pl.ds(start, rows)] * scale
            start = pl.multiple_of(2 * BLK + (spot + 1 - core) * rows, rows)
            give_done[2, part, hop] = (acc[pl.ds(start, rows)] * scale).astype(jnp.bfloat16)
    stores += [(keep_done, pair_keep), (give_done, pair_give)]
    copies = [
        pltpu.make_async_copy(source, target, out_sem.at[i])
        for i, (source, target) in enumerate(stores)
    ]
    for copy in copies:
        copy.start()
    for copy in copies:
        copy.wait()


def attend(meta, queries, grads, deltas, pack, pairs, twins, sizes):
    heads, rows, feature = sizes
    low, wide = jnp.bfloat16, jnp.float32
    part = (3, 2, 2, rows, feature)
    anywhere = pl.BlockSpec(memory_space=pl.ANY)
    work = 2 * heads * rows * (2 * BLK + 3 * rows) * feature * 10
    results = pl.pallas_call(
        functools.partial(attend_kernel, sizes),
        out_shape=[jax.ShapeDtypeStruct((heads, rows, feature), low)] * 2
        + [jax.ShapeDtypeStruct(part, wide), jax.ShapeDtypeStruct(part, low)],
        in_specs=[pl.BlockSpec(memory_space=pltpu.SMEM)] + [anywhere] * 6,
        out_specs=[anywhere] * 4,
        scratch_shapes=[
            pltpu.VMEM((2, heads, rows, feature), low),
            pltpu.VMEM((2, heads, rows, feature), low),
            pltpu.VMEM((2, 16, rows), low),
            pltpu.VMEM((2, 16, rows), wide),
            pltpu.VMEM((3, 2, 4, rows, feature), low),
            pltpu.VMEM((3 * BLK, feature), wide),
            pltpu.VMEM((3 * BLK, feature), wide),
            pltpu.VMEM((2, heads, rows, feature), low),
            pltpu.VMEM(part, wide),
            pltpu.VMEM(part, low),
            pltpu.SemaphoreType.DMA((14,)),
            pltpu.SemaphoreType.DMA((4,)),
        ],
        cost_estimate=pl.CostEstimate(
            flops=2 * work,
            bytes_accessed=8 * 1024 * 1024,
            transcendentals=work // (10 * feature),
        ),
        compiler_params=pltpu.CompilerParams(vmem_limit_bytes=48 * 1024 * 1024),
    )(meta, queries, grads, deltas, pack, pairs, twins)
    return results[:2], results[2], results[3]


def settle_kernel(heads, meta, *refs):
    query_parts, pair_parts = refs[:4], refs[4:8]
    query_out, key_out, value_out, sems = refs[8:]
    side = meta[0]
    copies = []
    for chunk in range(2):
        for hop in range(2):
            owner = 2 * (side ^ hop) + chunk
            place = 2 * chunk + hop
            for source, target in (
                (query_parts[place], query_out.at[0, pl.ds(owner * heads, heads)]),
                (pair_parts[place].at[0], key_out.at[0, owner]),
                (pair_parts[place].at[1], value_out.at[0, owner]),
            ):
                copy = pltpu.make_async_copy(source, target, sems.at[len(copies)])
                copy.start()
                copies.append(copy)
    for copy in copies:
        copy.wait()


def settle(meta, query_parts, pair_parts, shapes):
    heads = query_parts[0].shape[0]
    anywhere = pl.BlockSpec(memory_space=pl.ANY)
    return pl.pallas_call(
        functools.partial(settle_kernel, heads),
        out_shape=[jax.ShapeDtypeStruct(shape, jnp.bfloat16) for shape in shapes],
        in_specs=[pl.BlockSpec(memory_space=pltpu.SMEM)]
        + [pl.BlockSpec(memory_space=pltpu.VMEM)] * 8,
        out_specs=[anywhere] * 3,
        scratch_shapes=[pltpu.SemaphoreType.DMA((12,))],
    )(meta, *query_parts, *pair_parts)


def on_device(queries, key_states, value_states, outputs, out_grads, selected):
    devices = lax.axis_size("seq")
    sections = lax.axis_size("pipe")
    head_count, rows, feature = queries.shape[1:]
    key_heads = key_states.shape[1]
    members = BLK // rows
    heads = head_count // key_heads
    reach = devices // members - 1
    assert members == 4 and key_heads == 4 and heads <= 16
    rank = lax.axis_index("seq")
    block = rank // members
    side = rank // 2 % 2
    core = rank % 2

    def around(tensor, hop):
        return lax.ppermute(tensor, "seq", [(i, i ^ hop) for i in range(devices)])

    def along(tensor, hop):
        step = members * hop
        route = [(i, i + step) for i in range(devices) if 0 <= i + step < devices]
        return lax.ppermute(tensor, "seq", route)

    def previous(tensor, hop):
        route = [
            (i * sections + s, (i ^ 2 * hop) * sections + s - 1)
            for i in range(devices)
            for s in range(1, sections)
        ]
        return lax.ppermute(tensor, ("seq", "pipe"), route)

    def offsets_of(head):
        chosen = lax.dynamic_slice(selected, (0, block, head, 0), (1, 1, 1, 2)).reshape(2)
        return jnp.where(chosen < block, block - chosen, 0).astype(jnp.int32)

    offsets = [offsets_of(2 * side + chunk) for chunk in range(2)]

    def pair_of(which):
        return jnp.stack(
            [
                lax.dynamic_slice_in_dim(states[0], 2 * which, 2, 0)
                for states in (key_states, value_states)
            ],
            axis=1,
        )

    mine, other = pair_of(side), around(pair_of(1 - side), 2)
    near = [jnp.stack([mine[chunk], other[chunk]], axis=1) for chunk in range(2)]

    deltas = jnp.sum(
        out_grads[0].astype(jnp.float32) * outputs[0].astype(jnp.float32), axis=-1
    ).astype(jnp.bfloat16)
    deltas = deltas.reshape(key_heads, heads, rows)
    deltas = jnp.pad(deltas, ((0, 0), (0, 16 - heads), (0, 0)))

    def pack_of(head):
        query_part = lax.dynamic_slice_in_dim(queries[0], head * heads, heads, 0)
        grad_part = lax.dynamic_slice_in_dim(out_grads[0], head * heads, heads, 0)
        delta_part = lax.dynamic_index_in_dim(deltas, head, axis=0, keepdims=True)
        delta_part = jnp.pad(delta_part, ((0, 0), (0, rows - 16), (0, 0)))
        return jnp.concatenate([query_part, grad_part, delta_part], axis=0)

    packs = [around(pack_of(2 * (1 - side) + chunk), 2) for chunk in range(2)]
    sizes = (heads, rows, feature)
    query_back, pair_back = [], []
    for chunk in range(2):
        pairs = jnp.stack(
            [near[chunk]] + [along(near[chunk], hop) for hop in range(1, reach + 1)], axis=0
        )
        twins = around(pairs, 1)
        meta = jnp.concatenate([jnp.stack([side, core, 2 * side + chunk]), offsets[chunk]])
        query_parts, keep, give = attend(
            meta, queries, out_grads, deltas, packs[chunk], pairs, twins, sizes
        )
        query_back += [previous(part, hop) for hop, part in enumerate(query_parts)]
        partial = keep + around(give, 1).astype(jnp.float32)
        summed = partial[2]
        for hop in range(1, reach + 1):
            part = jnp.where(
                offsets[chunk][0] == hop,
                partial[0],
                jnp.where(offsets[chunk][1] == hop, partial[1], 0.0),
            )
            summed = summed + along(part.astype(jnp.bfloat16), -hop).astype(jnp.float32)
        summed = summed.astype(jnp.bfloat16)
        pair_back += [previous(summed[:, hop], hop) for hop in range(2)]
    shapes = (queries.shape, key_states.shape, value_states.shape)
    return tuple(settle(jnp.stack([side, core]), query_back, pair_back, shapes))


def solution(mesh):
    return jax.shard_map(
        on_device,
        mesh=mesh,
        in_specs=(
            P("pipe", None, "seq", None),
            P("pipe", None, "seq", None),
            P("pipe", None, "seq", None),
            P("pipe", None, "seq", None),
            P("pipe", None, "seq", None),
            P("pipe", None, None, None),
        ),
        out_specs=(
            P("pipe", None, "seq", None),
            P("pipe", None, "seq", None),
            P("pipe", None, "seq", None),
        ),
        check_vma=False,
    )
```

time: 114 us -> 128 us (1.12)
  the two profiles are of different devices: /device:TPU:16 before, /device:TPU:8 now
where the time goes in v3:
time: 128 us; the launch traced here: 127 us
  starting transfers between devices  43.2 us (34%)
  Pallas kernels  32.8 us (26%)
  waiting for transfers between devices  32.2 us (25%)
  between operations  9.1 us (7%)
  other arithmetic  6.51 us (5%)
  local copies, waits for them, and re-layouts  3.37 us (3%)
    pallas_call x2, Pallas kernels, attend(): pl.pallas_call(functools.partial(attend_kernel, sizes), out_shape=[jax.Sh...  30.5 us
    ppermute x12, starting transfers between devices, along(): return lax.ppermute(tensor, 'seq', route)  28.4 us
    ppermute x8, waiting for transfers between devices, previous(): return lax.ppermute(tensor, ('seq', 'pipe'), route)  16.3 us
    ppermute x12, waiting for transfers between devices, along(): return lax.ppermute(tensor, 'seq', route)  15.8 us
    ppermute x8, starting transfers between devices, previous(): return lax.ppermute(tensor, ('seq', 'pipe'), route)  10.3 us
    ppermute x7, starting transfers between devices, around(): return lax.ppermute(tensor, 'seq', [(i, i ^ hop) for i in range(devices)])  4.43 us
  transfers between devices with their start and end apart: 27, of which 5 were waited for; matrix products, arithmetic and copies ran while one was open for 6% of the time, Pallas kernels for 24%

profile of v3, /device:TPU:8, one launch (start us, length us, event | category | flops | bytes accessed | tf_op | source)
XLA Modules:
  0.0 127.2 jit_solution(5886583037526592810)
XLA Ops:
  0.7 1.0 dynamic-slice_bitcast_fusion.6
  1.7 1.6 %collective-permute-start.1 = (bf16[2,2,128,128]{3,2,1,0:T(8,128)(2,1)S(1)}, bf16[2,2,128,128]{3,2,1,0:T(8,128)(2,1)}, u32[]{:S(2)}, u32[]{:S(2)}) collective-permute-start(bf16[2,2,128,128]{3,2,1,0:T(8,128)(2,1)S(1)} %pad_maximum_fusion.2), channel_id=1, source_target_pairs={{0,4},{2,6},{4,0},{6,2},{8,12},{10,14},{12,8},{14,10},{16,20},{18,... | collective-permute-start | bytes 393224 | tf_op jit(solution)/shard_map/ppermute | solution.py:232
  3.2 2.3 %multiply_reduce_fusion = bf16[32,128]{1,0:T(8,128)(2,1)S(1)} fusion(bf16[1,32,128,128]{3,2,1,0:T(8,128)(2,1)} %param.9, bf16[1,32,128,128]{3,2,1,0:T(8,128)(2,1)} %grads.3), kind=kLoop, calls=%fused_computation | loop fusion | flops 2093056 | bytes 2105344 | tf_op jit(solution)/shard_map/reduce_sum | solution.py:265
  5.6 0.1 dynamic-slice_bitcast_fusion
  5.7 0.0 copy-start.10
  5.7 0.9 fusion.3
  6.6 0.5 collective-permute-start.8
  7.1 0.9 slice_bitcast_fusion.6
  8.0 0.7 fusion.21
  8.7 3.5 %collective-permute-start.9 = (bf16[2,2,128,128]{3,2,1,0:T(8,128)(2,1)}, bf16[2,2,128,128]{3,2,1,0:T(8,128)(2,1)}, u32[]{:S(2)}, u32[]{:S(2)}) collective-permute-start(bf16[2,2,128,128]{3,2,1,0:T(8,128)(2,1)} %get-tuple-element.38), channel_id=1, source_target_pairs={{0,8},{2,10},{4,12},{6,14},{8,16},{10,18},{12,20},{14,22},{16,24},... | collective-permute-start | bytes 393224 | tf_op jit(solution)/shard_map/ppermute | solution.py:237
  12.2 3.0 %collective-permute-start.10 = (bf16[2,2,128,128]{3,2,1,0:T(8,128)(2,1)}, bf16[2,2,128,128]{3,2,1,0:T(8,128)(2,1)}, u32[]{:S(2)}, u32[]{:S(2)}) collective-permute-start(bf16[2,2,128,128]{3,2,1,0:T(8,128)(2,1)} %get-tuple-element.38), channel_id=1, source_target_pairs={{0,16},{2,18},{4,20},{6,22},{8,24},{10,26},{12,28},{14,30},{1,17},... | collective-permute-start | bytes 393224 | tf_op jit(solution)/shard_map/ppermute | solution.py:237
  15.1 1.3 %collective-permute-start.11 = (bf16[2,2,128,128]{3,2,1,0:T(8,128)(2,1)}, bf16[2,2,128,128]{3,2,1,0:T(8,128)(2,1)}, u32[]{:S(2)}, u32[]{:S(2)}) collective-permute-start(bf16[2,2,128,128]{3,2,1,0:T(8,128)(2,1)} %get-tuple-element.38), channel_id=1, source_target_pairs={{0,24},{2,26},{4,28},{6,30},{1,25},{3,27},{5,29},{7,31}} | collective-permute-start | bytes 393224 | tf_op jit(solution)/shard_map/ppermute | solution.py:237
  16.4 0.2 fusion.23
  16.7 0.6 fusion.25
  17.3 6.1 %collective-permute-done.10 = bf16[2,2,128,128]{3,2,1,0:T(8,128)(2,1)} collective-permute-done((bf16[2,2,128,128]{3,2,1,0:T(8,128)(2,1)}, bf16[2,2,128,128]{3,2,1,0:T(8,128)(2,1)}, u32[]{:S(2)}, u32[]{:S(2)}) %collective-permute-start.10) | collective-permute-done | bytes 131104 | tf_op jit(solution)/shard_map/ppermute | solution.py:237
  23.4 0.0 collective-permute-done.11
  23.4 1.1 pad_maximum_fusion.1.pairs
  24.5 0.1 collective-permute-start.12
  24.6 0.1 pad_add_fusion.3.meta
  24.7 1.9 %collective-permute-start.2 = (bf16[2,2,128,128]{3,2,0,1:T(8,128)(2,1)S(1)}, bf16[2,2,128,128]{3,2,0,1:T(8,128)(2,1)S(1)}, u32[]{:S(2)}, u32[]{:S(2)}) collective-permute-start(bf16[2,2,128,128]{3,2,0,1:T(8,128)(2,1)S(1)} %get-tuple-element.44), channel_id=1, source_target_pairs={{0,8},{2,10},{4,12},{6,14},{8,16},{10,18},{12,20},{14,22},{16,24},... | collective-permute-start | bytes 393224 | tf_op jit(solution)/shard_map/ppermute | solution.py:237
  26.6 4.7 %collective-permute-start.3 = (bf16[2,2,128,128]{3,2,0,1:T(8,128)(2,1)S(1)}, bf16[2,2,128,128]{3,2,0,1:T(8,128)(2,1)S(1)}, u32[]{:S(2)}, u32[]{:S(2)}) collective-permute-start(bf16[2,2,128,128]{3,2,0,1:T(8,128)(2,1)S(1)} %get-tuple-element.44), channel_id=1, source_target_pairs={{0,16},{2,18},{4,20},{6,22},{8,24},{10,26},{12,28},{14,30},{1,17},... | collective-permute-start | bytes 393224 | tf_op jit(solution)/shard_map/ppermute | solution.py:237
  31.3 0.7 collective-permute-start.4
  31.9 0.1 pad_add_fusion.1.meta
  39.9 0.1 fusion.2
  39.9 0.0 collective-permute-done.2
  40.0 1.6 %collective-permute-start = (bf16[17,128,128]{2,1,0:T(8,128)(2,1)S(1)}, bf16[17,128,128]{2,1,0:T(8,128)(2,1)S(1)}, u32[]{:S(2)}, u32[]{:S(2)}) collective-permute-start(bf16[17,128,128]{2,1,0:T(8,128)(2,1)S(1)} %fusion.2), channel_id=1, source_target_pairs={{0,4},{2,6},{4,0},{6,2},{8,12},{10,14},{12,8},{14,10},{16,20},{18,... | collective-permute-start | bytes 1671176 | tf_op jit(solution)/shard_map/ppermute | solution.py:232
  41.5 0.0 collective-permute-done.4
  41.5 0.1 pad_maximum_fusion
  41.6 0.1 collective-permute-start.5
  41.7 0.0 collective-permute-done.8.pack
  41.7 15.2 %shard_map.86 = (bf16[8,128,128]{2,1,0:T(8,128)(2,1)S(1)}, bf16[8,128,128]{2,1,0:T(8,128)(2,1)S(1)}, f32[3,2,2,128,128]{4,3,2,1,0:T(8,128)S(1)}, bf16[3,2,2,128,128]{4,3,2,1,0:T(8,128)(2,1)S(1)}) custom-call(s32[5]{0:T(128)S(1)} %pad_add_fusion.3.meta, bf16[1,32,128,128]{3,2,1,0:T(8,128)(2,1)S(1)} %copy-done.1, bf16[1,32,128,128]{3,2,1,0:T(8,128)(2,1)S(1)} %copy-done, ...), custom_call_target="tpu_custom_call" | custom-call | flops 7381975040 | bytes 8388608 | tf_op jit(solution)/shard_map/pallas_call | solution.py:153
  57.0 0.6 collective-permute-start.21
  57.6 0.0 collective-permute-done.5
  57.6 0.0 collective-permute-done.pack
  57.6 15.2 %shard_map.85 = (bf16[8,128,128]{2,1,0:T(8,128)(2,1)S(1)}, bf16[8,128,128]{2,1,0:T(8,128)(2,1)S(1)}, f32[3,2,2,128,128]{4,3,2,1,0:T(8,128)S(1)}, bf16[3,2,2,128,128]{4,3,2,1,0:T(8,128)(2,1)S(1)}) custom-call(s32[5]{0:T(128)S(1)} %pad_add_fusion.1.meta, bf16[1,32,128,128]{3,2,1,0:T(8,128)(2,1)S(1)} %copy-done.1, bf16[1,32,128,128]{3,2,1,0:T(8,128)(2,1)S(1)} %copy-done, ...), custom_call_target="tpu_custom_call" | custom-call | flops 7381975040 | bytes 8388608 | tf_op jit(solution)/shard_map/pallas_call | solution.py:153
  72.9 0.1 collective-permute-start.15
  73.0 1.3 %collective-permute-start.13 = (bf16[8,128,128]{2,1,0:T(8,128)(2,1)S(1)}, bf16[8,128,128]{2,1,0:T(8,128)(2,1)S(1)}, u32[]{:S(2)}, u32[]{:S(2)}) collective-permute-start(bf16[8,128,128]{2,1,0:T(8,128)(2,1)S(1)} %get-tuple-element.13), channel_id=1, source_target_pairs={{1,0},{3,2},{5,4},{7,6},{9,8},{11,10},{13,12},{15,14},{17,16},{19,... | collective-permute-start | bytes 786440 | tf_op jit(solution)/shard_map/ppermute | solution.py:245
  74.3 1.3 %collective-permute-start.14 = (bf16[8,128,128]{2,1,0:T(8,128)(2,1)S(1)}, bf16[8,128,128]{2,1,0:T(8,128)(2,1)S(1)}, u32[]{:S(2)}, u32[]{:S(2)}) collective-permute-start(bf16[8,128,128]{2,1,0:T(8,128)(2,1)S(1)} %get-tuple-element.14), channel_id=1, source_target_pairs={{1,4},{3,6},{5,0},{7,2},{9,12},{11,14},{13,8},{15,10},{17,20},{19,... | collective-permute-start | bytes 786440 | tf_op jit(solution)/shard_map/ppermute | solution.py:245
  75.6 0.0 collective-permute-done.21
  75.6 0.1 copy_add_fusion
  75.7 0.1 fusion.15
  75.8 5.2 %collective-permute-start.22 = (bf16[2,2,128,128]{3,2,0,1:T(8,128)(2,1)S(1)}, bf16[2,2,128,128]{3,2,0,1:T(8,128)(2,1)S(1)}, u32[]{:S(2)}, u32[]{:S(2)}) collective-permute-start(bf16[2,2,128,128]{3,2,0,1:T(8,128)(2,1)S(1)} %get-tuple-element.27), channel_id=1, source_target_pairs={{8,0},{10,2},{12,4},{14,6},{16,8},{18,10},{20,12},{22,14},{24,16},... | collective-permute-start | bytes 393224 | tf_op jit(solution)/shard_map/ppermute | solution.py:237
  81.0 1.3 %collective-permute-start.23 = (bf16[2,2,128,128]{3,2,0,1:T(8,128)(2,1)S(1)}, bf16[2,2,128,128]{3,2,0,1:T(8,128)(2,1)S(1)}, u32[]{:S(2)}, u32[]{:S(2)}) collective-permute-start(bf16[2,2,128,128]{3,2,0,1:T(8,128)(2,1)S(1)} %get-tuple-element.29), channel_id=1, source_target_pairs={{16,0},{18,2},{20,4},{22,6},{24,8},{26,10},{28,12},{30,14},{17,1},... | collective-permute-start | bytes 393224 | tf_op jit(solution)/shard_map/ppermute | solution.py:237
  82.3 0.7 collective-permute-start.24
  83.0 0.1 copy_add_fusion.1
  83.0 0.1 fusion.12
  83.1 3.1 %collective-permute-done.22 = bf16[2,2,128,128]{3,2,0,1:T(8,128)(2,1)S(1)} collective-permute-done((bf16[2,2,128,128]{3,2,0,1:T(8,128)(2,1)S(1)}, bf16[2,2,128,128]{3,2,0,1:T(8,128)(2,1)S(1)}, u32[]{:S(2)}, u32[]{:S(2)}) %collective-permute-start.22) | collective-permute-done | bytes 131104 | tf_op jit(solution)/shard_map/ppermute | solution.py:237
  86.2 4.3 %collective-permute-start.16 = (bf16[2,2,128,128]{3,2,0,1:T(8,128)(2,1)S(1)}, bf16[2,2,128,128]{3,2,0,1:T(8,128)(2,1)S(1)}, u32[]{:S(2)}, u32[]{:S(2)}) collective-permute-start(bf16[2,2,128,128]{3,2,0,1:T(8,128)(2,1)S(1)} %get-tuple-element.30), channel_id=1, source_target_pairs={{8,0},{10,2},{12,4},{14,6},{16,8},{18,10},{20,12},{22,14},{24,16},... | collective-permute-start | bytes 393224 | tf_op jit(solution)/shard_map/ppermute | solution.py:237
  90.6 1.3 %collective-permute-start.17 = (bf16[2,2,128,128]{3,2,0,1:T(8,128)(2,1)S(1)}, bf16[2,2,128,128]{3,2,0,1:T(8,128)(2,1)S(1)}, u32[]{:S(2)}, u32[]{:S(2)}) collective-permute-start(bf16[2,2,128,128]{3,2,0,1:T(8,128)(2,1)S(1)} %get-tuple-element.32), channel_id=1, source_target_pairs={{16,0},{18,2},{20,4},{22,6},{24,8},{26,10},{28,12},{30,14},{17,1},... | collective-permute-start | bytes 393224 | tf_op jit(solution)/shard_map/ppermute | solution.py:237
  91.9 0.7 collective-permute-start.18
  92.6 0.1 fusion.7
  92.7 6.6 %collective-permute-done.16 = bf16[2,2,128,128]{3,2,0,1:T(8,128)(2,1)S(1)} collective-permute-done((bf16[2,2,128,128]{3,2,0,1:T(8,128)(2,1)S(1)}, bf16[2,2,128,128]{3,2,0,1:T(8,128)(2,1)S(1)}, u32[]{:S(2)}, u32[]{:S(2)}) %collective-permute-start.16) | collective-permute-done | bytes 131104 | tf_op jit(solution)/shard_map/ppermute | solution.py:237
  99.3 1.3 %collective-permute-start.6 = (bf16[8,128,128]{2,1,0:T(8,128)(2,1)S(1)}, bf16[8,128,128]{2,1,0:T(8,128)(2,1)S(1)}, u32[]{:S(2)}, u32[]{:S(2)}) collective-permute-start(bf16[8,128,128]{2,1,0:T(8,128)(2,1)S(1)} %get-tuple-element.11), channel_id=1, source_target_pairs={{1,0},{3,2},{5,4},{7,6},{9,8},{11,10},{13,12},{15,14},{17,16},{19,... | collective-permute-start | bytes 786440 | tf_op jit(solution)/shard_map/ppermute | solution.py:245
  100.5 1.3 %collective-permute-start.7 = (bf16[8,128,128]{2,1,0:T(8,128)(2,1)S(1)}, bf16[8,128,128]{2,1,0:T(8,128)(2,1)S(1)}, u32[]{:S(2)}, u32[]{:S(2)}) collective-permute-start(bf16[8,128,128]{2,1,0:T(8,128)(2,1)S(1)} %get-tuple-element.12), channel_id=1, source_target_pairs={{1,4},{3,6},{5,0},{7,2},{9,12},{11,14},{13,8},{15,10},{17,20},{19,... | collective-permute-start | bytes 786440 | tf_op jit(solution)/shard_map/ppermute | solution.py:245
  101.9 1.3 %collective-permute-start.25 = (bf16[2,128,128]{2,1,0:T(8,128)(2,1)S(1)}, bf16[2,128,128]{2,1,0:T(8,128)(2,1)S(1)}, u32[]{:S(2)}, u32[]{:S(2)}) collective-permute-start(bf16[2,128,128]{2,1,0:T(8,128)(2,1)S(1)} %get-tuple-element.34), channel_id=1, source_target_pairs={{1,0},{3,2},{5,4},{7,6},{9,8},{11,10},{13,12},{15,14},{17,16},{19,... | collective-permute-start | bytes 196616 | tf_op jit(solution)/shard_map/ppermute | solution.py:245
  103.2 0.1 fusion.11
  103.3 1.3 %collective-permute-start.26 = (bf16[2,128,128]{2,1,0:T(8,128)(2,1)S(1)}, bf16[2,128,128]{2,1,0:T(8,128)(2,1)S(1)}, u32[]{:S(2)}, u32[]{:S(2)}) collective-permute-start(bf16[2,128,128]{2,1,0:T(8,128)(2,1)S(1)} %get-tuple-element.33), channel_id=1, source_target_pairs={{1,4},{3,6},{5,0},{7,2},{9,12},{11,14},{13,8},{15,10},{17,20},{19,... | collective-permute-start | bytes 196616 | tf_op jit(solution)/shard_map/ppermute | solution.py:245
  104.6 1.3 %collective-permute-start.19 = (bf16[2,128,128]{2,1,0:T(8,128)(2,1)S(1)}, bf16[2,128,128]{2,1,0:T(8,128)(2,1)S(1)}, u32[]{:S(2)}, u32[]{:S(2)}) collective-permute-start(bf16[2,128,128]{2,1,0:T(8,128)(2,1)S(1)} %get-tuple-element.36), channel_id=1, source_target_pairs={{1,0},{3,2},{5,4},{7,6},{9,8},{11,10},{13,12},{15,14},{17,16},{19,... | collective-permute-start | bytes 196616 | tf_op jit(solution)/shard_map/ppermute | solution.py:245
  105.9 11.2 %collective-permute-done.6.refs_0_ = bf16[8,128,128]{2,1,0:T(8,128)(2,1)S(1)} collective-permute-done((bf16[8,128,128]{2,1,0:T(8,128)(2,1)S(1)}, bf16[8,128,128]{2,1,0:T(8,128)(2,1)S(1)}, u32[]{:S(2)}, u32[]{:S(2)}) %collective-permute-start.6) | collective-permute-done | bytes 262176 | tf_op jit(solution)/shard_map/ppermute | solution.py:245
  117.1 1.3 %collective-permute-start.20 = (bf16[2,128,128]{2,1,0:T(8,128)(2,1)S(1)}, bf16[2,128,128]{2,1,0:T(8,128)(2,1)S(1)}, u32[]{:S(2)}, u32[]{:S(2)}) collective-permute-start(bf16[2,128,128]{2,1,0:T(8,128)(2,1)S(1)} %get-tuple-element.35), channel_id=1, source_target_pairs={{1,4},{3,6},{5,0},{7,2},{9,12},{11,14},{13,8},{15,10},{17,20},{19,... | collective-permute-start | bytes 196616 | tf_op jit(solution)/shard_map/ppermute | solution.py:245
  118.4 0.6 pad_add_fusion.meta
  119.0 5.1 %collective-permute-done.20.refs_5_ = bf16[2,128,128]{2,1,0:T(8,128)(2,1)S(1)} collective-permute-done((bf16[2,128,128]{2,1,0:T(8,128)(2,1)S(1)}, bf16[2,128,128]{2,1,0:T(8,128)(2,1)S(1)}, u32[]{:S(2)}, u32[]{:S(2)}) %collective-permute-start.20) | collective-permute-done | bytes 65568 | tf_op jit(solution)/shard_map/ppermute | solution.py:245
  124.2 0.6 copy-done.9
  124.8 2.4 %shard_map.87 = (bf16[1,32,128,128]{3,2,1,0:T(8,128)(2,1)}, bf16[1,4,128,128]{3,2,1,0:T(8,128)(2,1)}, bf16[1,4,128,128]{3,2,1,0:T(8,128)(2,1)}) custom-call(s32[2]{0:T(128)} %pad_add_fusion.meta, bf16[8,128,128]{2,1,0:T(8,128)(2,1)} %copy-done.4, bf16[8,128,128]{2,1,0:T(8,128)(2,1)} %copy-done.5, bf16[8,128,128]{2,1,0:T(8,128)(2,1)} %copy-done.2, ...), custom_call_target="tpu_custom_call" | custom-call | tf_op jit(solution)/shard_map/pallas_call | solution.py:207
  (46 shorter events, 0.3 us)
Async XLA Ops:
  1.7 5.5 %collective-permute-start.1 = (bf16[2,2,128,128]{3,2,1,0:T(8,128)(2,1)S(1)}, bf16[2,2,128,128]{3,2,1,0:T(8,128)(2,1)}, u32[]{:S(2)}, u32[]{:S(2)}) collective-permute-start(bf16[2,2,128,128]{3,2,1,0:T(8,128)(2,1)S(1)} %pad_maximum_fusion.2), channel_id=1, source_target_pairs={{0,4},{2,6},{4,0},{6,2},{8,12},{10,14},{12,8},{14,10},{16,20},{18,... | collective-permute-start | bytes 393224 | tf_op jit(solution)/shard_map/ppermute | solution.py:232
  3.2 2.3 %copy-start = (bf16[1,32,128,128]{3,2,1,0:T(8,128)(2,1)S(1)}, bf16[1,32,128,128]{3,2,1,0:T(8,128)(2,1)}, u32[]{:S(2)}) copy-start(bf16[1,32,128,128]{3,2,1,0:T(8,128)(2,1)} %grads.3) | copy-start | bytes 3145732
  3.2 2.3 %copy-start.1 = (bf16[1,32,128,128]{3,2,1,0:T(8,128)(2,1)S(1)}, bf16[1,32,128,128]{3,2,1,0:T(8,128)(2,1)}, u32[]{:S(2)}) copy-start(bf16[1,32,128,128]{3,2,1,0:T(8,128)(2,1)} %queries.3) | copy-start | bytes 3145732
  5.7 10.7 %copy-start.10 = (s32[1,4,4,2]{2,3,1,0:T(2,128)S(1)}, s32[1,4,4,2]{2,3,1,0:T(2,128)}, u32[]{:S(2)}) copy-start(s32[1,4,4,2]{2,3,1,0:T(2,128)} %param.11) | copy-start | bytes 388
  6.6 35.2 %collective-permute-start.8 = (bf16[17,128,128]{2,1,0:T(8,128)(2,1)}, bf16[17,128,128]{2,1,0:T(8,128)(2,1)S(1)}, u32[]{:S(2)}, u32[]{:S(2)}) collective-permute-start(bf16[17,128,128]{2,1,0:T(8,128)(2,1)} %fusion.3), channel_id=1, source_target_pairs={{0,4},{2,6},{4,0},{6,2},{8,12},{10,14},{12,8},{14,10},{16,20},{18,... | collective-permute-start | bytes 1671176 | tf_op jit(solution)/shard_map/ppermute | solution.py:232
  8.7 8.6 %collective-permute-start.9 = (bf16[2,2,128,128]{3,2,1,0:T(8,128)(2,1)}, bf16[2,2,128,128]{3,2,1,0:T(8,128)(2,1)}, u32[]{:S(2)}, u32[]{:S(2)}) collective-permute-start(bf16[2,2,128,128]{3,2,1,0:T(8,128)(2,1)} %get-tuple-element.38), channel_id=1, source_target_pairs={{0,8},{2,10},{4,12},{6,14},{8,16},{10,18},{12,20},{14,22},{16,24},... | collective-permute-start | bytes 393224 | tf_op jit(solution)/shard_map/ppermute | solution.py:237
  12.2 11.2 %collective-permute-start.10 = (bf16[2,2,128,128]{3,2,1,0:T(8,128)(2,1)}, bf16[2,2,128,128]{3,2,1,0:T(8,128)(2,1)}, u32[]{:S(2)}, u32[]{:S(2)}) collective-permute-start(bf16[2,2,128,128]{3,2,1,0:T(8,128)(2,1)} %get-tuple-element.38), channel_id=1, source_target_pairs={{0,16},{2,18},{4,20},{6,22},{8,24},{10,26},{12,28},{14,30},{1,17},... | collective-permute-start | bytes 393224 | tf_op jit(solution)/shard_map/ppermute | solution.py:237
  15.1 8.3 %collective-permute-start.11 = (bf16[2,2,128,128]{3,2,1,0:T(8,128)(2,1)}, bf16[2,2,128,128]{3,2,1,0:T(8,128)(2,1)}, u32[]{:S(2)}, u32[]{:S(2)}) collective-permute-start(bf16[2,2,128,128]{3,2,1,0:T(8,128)(2,1)} %get-tuple-element.38), channel_id=1, source_target_pairs={{0,24},{2,26},{4,28},{6,30},{1,25},{3,27},{5,29},{7,31}} | collective-permute-start | bytes 393224 | tf_op jit(solution)/shard_map/ppermute | solution.py:237
  24.5 17.2 %collective-permute-start.12 = (bf16[4,2,2,128,128]{4,3,2,1,0:T(8,128)(2,1)S(1)}, bf16[4,2,2,128,128]{4,3,2,1,0:T(8,128)(2,1)S(1)}, u32[]{:S(2)}, u32[]{:S(2)}) collective-permute-start(bf16[4,2,2,128,128]{4,3,2,1,0:T(8,128)(2,1)S(1)} %pad_maximum_fusion.1.pairs), channel_id=1, source_target_pairs={{0,2},{2,0},{4,6},{6,4},{8,10},{10,8},{12,14},{14,12},{16,18},{18,... | collective-permute-start | bytes 1572872 | tf_op jit(solution)/shard_map/ppermute | solution.py:232
  24.7 15.3 %collective-permute-start.2 = (bf16[2,2,128,128]{3,2,0,1:T(8,128)(2,1)S(1)}, bf16[2,2,128,128]{3,2,0,1:T(8,128)(2,1)S(1)}, u32[]{:S(2)}, u32[]{:S(2)}) collective-permute-start(bf16[2,2,128,128]{3,2,0,1:T(8,128)(2,1)S(1)} %get-tuple-element.44), channel_id=1, source_target_pairs={{0,8},{2,10},{4,12},{6,14},{8,16},{10,18},{12,20},{14,22},{16,24},... | collective-permute-start | bytes 393224 | tf_op jit(solution)/shard_map/ppermute | solution.py:237
  26.6 14.9 %collective-permute-start.3 = (bf16[2,2,128,128]{3,2,0,1:T(8,128)(2,1)S(1)}, bf16[2,2,128,128]{3,2,0,1:T(8,128)(2,1)S(1)}, u32[]{:S(2)}, u32[]{:S(2)}) collective-permute-start(bf16[2,2,128,128]{3,2,0,1:T(8,128)(2,1)S(1)} %get-tuple-element.44), channel_id=1, source_target_pairs={{0,16},{2,18},{4,20},{6,22},{8,24},{10,26},{12,28},{14,30},{1,17},... | collective-permute-start | bytes 393224 | tf_op jit(solution)/shard_map/ppermute | solution.py:237
  31.3 10.2 %collective-permute-start.4 = (bf16[2,2,128,128]{3,2,0,1:T(8,128)(2,1)S(1)}, bf16[2,2,128,128]{3,2,0,1:T(8,128)(2,1)S(1)}, u32[]{:S(2)}, u32[]{:S(2)}) collective-permute-start(bf16[2,2,128,128]{3,2,0,1:T(8,128)(2,1)S(1)} %get-tuple-element.44), channel_id=1, source_target_pairs={{0,24},{2,26},{4,28},{6,30},{1,25},{3,27},{5,29},{7,31}} | collective-permute-start | bytes 393224 | tf_op jit(solution)/shard_map/ppermute | solution.py:237
  40.0 17.7 %collective-permute-start = (bf16[17,128,128]{2,1,0:T(8,128)(2,1)S(1)}, bf16[17,128,128]{2,1,0:T(8,128)(2,1)S(1)}, u32[]{:S(2)}, u32[]{:S(2)}) collective-permute-start(bf16[17,128,128]{2,1,0:T(8,128)(2,1)S(1)} %fusion.2), channel_id=1, source_target_pairs={{0,4},{2,6},{4,0},{6,2},{8,12},{10,14},{12,8},{14,10},{16,20},{18,... | collective-permute-start | bytes 1671176 | tf_op jit(solution)/shard_map/ppermute | solution.py:232
  41.6 16.0 %collective-permute-start.5 = (bf16[4,2,2,128,128]{4,3,1,2,0:T(8,128)(2,1)S(1)}, bf16[4,2,2,128,128]{4,3,1,2,0:T(8,128)(2,1)S(1)}, u32[]{:S(2)}, u32[]{:S(2)}) collective-permute-start(bf16[4,2,2,128,128]{4,3,1,2,0:T(8,128)(2,1)S(1)} %pad_maximum_fusion), channel_id=1, source_target_pairs={{0,2},{2,0},{4,6},{6,4},{8,10},{10,8},{12,14},{14,12},{16,18},{18,... | collective-permute-start | bytes 1572872 | tf_op jit(solution)/shard_map/ppermute | solution.py:232
  57.0 18.6 %collective-permute-start.21 = (bf16[3,2,2,128,128]{4,3,1,2,0:T(8,128)(2,1)S(1)}, bf16[3,2,2,128,128]{4,3,1,2,0:T(8,128)(2,1)S(1)}, u32[]{:S(2)}, u32[]{:S(2)}) collective-permute-start(bf16[3,2,2,128,128]{4,3,1,2,0:T(8,128)(2,1)S(1)} %copy.14), channel_id=1, source_target_pairs={{0,2},{2,0},{4,6},{6,4},{8,10},{10,8},{12,14},{14,12},{16,18},{18,... | collective-permute-start | bytes 1179656 | tf_op jit(solution)/shard_map/ppermute | solution.py:232
  72.9 9.4 %collective-permute-start.15 = (bf16[3,2,2,128,128]{4,3,1,2,0:T(8,128)(2,1)S(1)}, bf16[3,2,2,128,128]{4,3,1,2,0:T(8,128)(2,1)S(1)}, u32[]{:S(2)}, u32[]{:S(2)}) collective-permute-start(bf16[3,2,2,128,128]{4,3,1,2,0:T(8,128)(2,1)S(1)} %copy.12), channel_id=1, source_target_pairs={{0,2},{2,0},{4,6},{6,4},{8,10},{10,8},{12,14},{14,12},{16,18},{18,... | collective-permute-start | bytes 1179656 | tf_op jit(solution)/shard_map/ppermute | solution.py:232
  73.0 30.3 %collective-permute-start.13 = (bf16[8,128,128]{2,1,0:T(8,128)(2,1)S(1)}, bf16[8,128,128]{2,1,0:T(8,128)(2,1)S(1)}, u32[]{:S(2)}, u32[]{:S(2)}) collective-permute-start(bf16[8,128,128]{2,1,0:T(8,128)(2,1)S(1)} %get-tuple-element.13), channel_id=1, source_target_pairs={{1,0},{3,2},{5,4},{7,6},{9,8},{11,10},{13,12},{15,14},{17,16},{19,... | collective-permute-start | bytes 786440 | tf_op jit(solution)/shard_map/ppermute | solution.py:245
  74.3 30.3 %collective-permute-start.14 = (bf16[8,128,128]{2,1,0:T(8,128)(2,1)S(1)}, bf16[8,128,128]{2,1,0:T(8,128)(2,1)S(1)}, u32[]{:S(2)}, u32[]{:S(2)}) collective-permute-start(bf16[8,128,128]{2,1,0:T(8,128)(2,1)S(1)} %get-tuple-element.14), channel_id=1, source_target_pairs={{1,4},{3,6},{5,0},{7,2},{9,12},{11,14},{13,8},{15,10},{17,20},{19,... | collective-permute-start | bytes 786440 | tf_op jit(solution)/shard_map/ppermute | solution.py:245
  75.8 10.5 %collective-permute-start.22 = (bf16[2,2,128,128]{3,2,0,1:T(8,128)(2,1)S(1)}, bf16[2,2,128,128]{3,2,0,1:T(8,128)(2,1)S(1)}, u32[]{:S(2)}, u32[]{:S(2)}) collective-permute-start(bf16[2,2,128,128]{3,2,0,1:T(8,128)(2,1)S(1)} %get-tuple-element.27), channel_id=1, source_target_pairs={{8,0},{10,2},{12,4},{14,6},{16,8},{18,10},{20,12},{22,14},{24,16},... | collective-permute-start | bytes 393224 | tf_op jit(solution)/shard_map/ppermute | solution.py:237
  81.0 9.6 %collective-permute-start.23 = (bf16[2,2,128,128]{3,2,0,1:T(8,128)(2,1)S(1)}, bf16[2,2,128,128]{3,2,0,1:T(8,128)(2,1)S(1)}, u32[]{:S(2)}, u32[]{:S(2)}) collective-permute-start(bf16[2,2,128,128]{3,2,0,1:T(8,128)(2,1)S(1)} %get-tuple-element.29), channel_id=1, source_target_pairs={{16,0},{18,2},{20,4},{22,6},{24,8},{26,10},{28,12},{30,14},{17,1},... | collective-permute-start | bytes 393224 | tf_op jit(solution)/shard_map/ppermute | solution.py:237
  82.3 9.6 %collective-permute-start.24 = (bf16[2,2,128,128]{3,2,0,1:T(8,128)(2,1)S(1)}, bf16[2,2,128,128]{3,2,0,1:T(8,128)(2,1)S(1)}, u32[]{:S(2)}, u32[]{:S(2)}) collective-permute-start(bf16[2,2,128,128]{3,2,0,1:T(8,128)(2,1)S(1)} %get-tuple-element.28), channel_id=1, source_target_pairs={{24,0},{26,2},{28,4},{30,6},{25,1},{27,3},{29,5},{31,7}} | collective-permute-start | bytes 393224 | tf_op jit(solution)/shard_map/ppermute | solution.py:237
  86.2 13.0 %collective-permute-start.16 = (bf16[2,2,128,128]{3,2,0,1:T(8,128)(2,1)S(1)}, bf16[2,2,128,128]{3,2,0,1:T(8,128)(2,1)S(1)}, u32[]{:S(2)}, u32[]{:S(2)}) collective-permute-start(bf16[2,2,128,128]{3,2,0,1:T(8,128)(2,1)S(1)} %get-tuple-element.30), channel_id=1, source_target_pairs={{8,0},{10,2},{12,4},{14,6},{16,8},{18,10},{20,12},{22,14},{24,16},... | collective-permute-start | bytes 393224 | tf_op jit(solution)/shard_map/ppermute | solution.py:237
  90.6 9.9 %collective-permute-start.17 = (bf16[2,2,128,128]{3,2,0,1:T(8,128)(2,1)S(1)}, bf16[2,2,128,128]{3,2,0,1:T(8,128)(2,1)S(1)}, u32[]{:S(2)}, u32[]{:S(2)}) collective-permute-start(bf16[2,2,128,128]{3,2,0,1:T(8,128)(2,1)S(1)} %get-tuple-element.32), channel_id=1, source_target_pairs={{16,0},{18,2},{20,4},{22,6},{24,8},{26,10},{28,12},{30,14},{17,1},... | collective-permute-start | bytes 393224 | tf_op jit(solution)/shard_map/ppermute | solution.py:237
  91.9 9.9 %collective-permute-start.18 = (bf16[2,2,128,128]{3,2,0,1:T(8,128)(2,1)S(1)}, bf16[2,2,128,128]{3,2,0,1:T(8,128)(2,1)S(1)}, u32[]{:S(2)}, u32[]{:S(2)}) collective-permute-start(bf16[2,2,128,128]{3,2,0,1:T(8,128)(2,1)S(1)} %get-tuple-element.31), channel_id=1, source_target_pairs={{24,0},{26,2},{28,4},{30,6},{25,1},{27,3},{29,5},{31,7}} | collective-permute-start | bytes 393224 | tf_op jit(solution)/shard_map/ppermute | solution.py:237
  99.3 17.8 %collective-permute-start.6 = (bf16[8,128,128]{2,1,0:T(8,128)(2,1)S(1)}, bf16[8,128,128]{2,1,0:T(8,128)(2,1)S(1)}, u32[]{:S(2)}, u32[]{:S(2)}) collective-permute-start(bf16[8,128,128]{2,1,0:T(8,128)(2,1)S(1)} %get-tuple-element.11), channel_id=1, source_target_pairs={{1,0},{3,2},{5,4},{7,6},{9,8},{11,10},{13,12},{15,14},{17,16},{19,... | collective-permute-start | bytes 786440 | tf_op jit(solution)/shard_map/ppermute | solution.py:245
  100.5 18.4 %collective-permute-start.7 = (bf16[8,128,128]{2,1,0:T(8,128)(2,1)S(1)}, bf16[8,128,128]{2,1,0:T(8,128)(2,1)S(1)}, u32[]{:S(2)}, u32[]{:S(2)}) collective-permute-start(bf16[8,128,128]{2,1,0:T(8,128)(2,1)S(1)} %get-tuple-element.12), channel_id=1, source_target_pairs={{1,4},{3,6},{5,0},{7,2},{9,12},{11,14},{13,8},{15,10},{17,20},{19,... | collective-permute-start | bytes 786440 | tf_op jit(solution)/shard_map/ppermute | solution.py:245
  101.9 17.1 %collective-permute-start.25 = (bf16[2,128,128]{2,1,0:T(8,128)(2,1)S(1)}, bf16[2,128,128]{2,1,0:T(8,128)(2,1)S(1)}, u32[]{:S(2)}, u32[]{:S(2)}) collective-permute-start(bf16[2,128,128]{2,1,0:T(8,128)(2,1)S(1)} %get-tuple-element.34), channel_id=1, source_target_pairs={{1,0},{3,2},{5,4},{7,6},{9,8},{11,10},{13,12},{15,14},{17,16},{19,... | collective-permute-start | bytes 196616 | tf_op jit(solution)/shard_map/ppermute | solution.py:245
  103.3 20.9 %copy-start.2 = (bf16[8,128,128]{2,1,0:T(8,128)(2,1)}, bf16[8,128,128]{2,1,0:T(8,128)(2,1)S(1)}, u32[]{:S(2)}) copy-start(bf16[8,128,128]{2,1,0:T(8,128)(2,1)S(1)} %collective-permute-done.13.refs_2_) | copy-start | bytes 786436
  103.3 15.7 %collective-permute-start.26 = (bf16[2,128,128]{2,1,0:T(8,128)(2,1)S(1)}, bf16[2,128,128]{2,1,0:T(8,128)(2,1)S(1)}, u32[]{:S(2)}, u32[]{:S(2)}) collective-permute-start(bf16[2,128,128]{2,1,0:T(8,128)(2,1)S(1)} %get-tuple-element.33), channel_id=1, source_target_pairs={{1,4},{3,6},{5,0},{7,2},{9,12},{11,14},{13,8},{15,10},{17,20},{19,... | collective-permute-start | bytes 196616 | tf_op jit(solution)/shard_map/ppermute | solution.py:245
  104.6 19.5 %copy-start.3 = (bf16[8,128,128]{2,1,0:T(8,128)(2,1)}, bf16[8,128,128]{2,1,0:T(8,128)(2,1)S(1)}, u32[]{:S(2)}) copy-start(bf16[8,128,128]{2,1,0:T(8,128)(2,1)S(1)} %collective-permute-done.14.refs_3_) | copy-start | bytes 786436
  104.6 14.4 %collective-permute-start.19 = (bf16[2,128,128]{2,1,0:T(8,128)(2,1)S(1)}, bf16[2,128,128]{2,1,0:T(8,128)(2,1)S(1)}, u32[]{:S(2)}, u32[]{:S(2)}) collective-permute-start(bf16[2,128,128]{2,1,0:T(8,128)(2,1)S(1)} %get-tuple-element.36), channel_id=1, source_target_pairs={{1,0},{3,2},{5,4},{7,6},{9,8},{11,10},{13,12},{15,14},{17,16},{19,... | collective-permute-start | bytes 196616 | tf_op jit(solution)/shard_map/ppermute | solution.py:245
  117.1 7.1 %copy-start.4 = (bf16[8,128,128]{2,1,0:T(8,128)(2,1)}, bf16[8,128,128]{2,1,0:T(8,128)(2,1)S(1)}, u32[]{:S(2)}) copy-start(bf16[8,128,128]{2,1,0:T(8,128)(2,1)S(1)} %collective-permute-done.6.refs_0_) | copy-start | bytes 786436
  117.1 7.0 %collective-permute-start.20 = (bf16[2,128,128]{2,1,0:T(8,128)(2,1)S(1)}, bf16[2,128,128]{2,1,0:T(8,128)(2,1)S(1)}, u32[]{:S(2)}, u32[]{:S(2)}) collective-permute-start(bf16[2,128,128]{2,1,0:T(8,128)(2,1)S(1)} %get-tuple-element.35), channel_id=1, source_target_pairs={{1,4},{3,6},{5,0},{7,2},{9,12},{11,14},{13,8},{15,10},{17,20},{19,... | collective-permute-start | bytes 196616 | tf_op jit(solution)/shard_map/ppermute | solution.py:245
  118.9 5.2 %copy-start.5 = (bf16[8,128,128]{2,1,0:T(8,128)(2,1)}, bf16[8,128,128]{2,1,0:T(8,128)(2,1)S(1)}, u32[]{:S(2)}) copy-start(bf16[8,128,128]{2,1,0:T(8,128)(2,1)S(1)} %collective-permute-done.7.refs_1_) | copy-start | bytes 786436
  118.9 5.2 %copy-start.6 = (bf16[2,128,128]{2,1,0:T(8,128)(2,1)}, bf16[2,128,128]{2,1,0:T(8,128)(2,1)S(1)}, u32[]{:S(2)}) copy-start(bf16[2,128,128]{2,1,0:T(8,128)(2,1)S(1)} %collective-permute-done.25.refs_6_) | copy-start | bytes 196612
  118.9 5.2 %copy-start.7 = (bf16[2,128,128]{2,1,0:T(8,128)(2,1)}, bf16[2,128,128]{2,1,0:T(8,128)(2,1)S(1)}, u32[]{:S(2)}) copy-start(bf16[2,128,128]{2,1,0:T(8,128)(2,1)S(1)} %collective-permute-done.26.refs_7_) | copy-start | bytes 196612
  119.0 5.2 %copy-start.8 = (bf16[2,128,128]{2,1,0:T(8,128)(2,1)}, bf16[2,128,128]{2,1,0:T(8,128)(2,1)S(1)}, u32[]{:S(2)}) copy-start(bf16[2,128,128]{2,1,0:T(8,128)(2,1)S(1)} %collective-permute-done.19.refs_4_) | copy-start | bytes 196612
  124.2 0.6 copy-start.9
